TPU v7x, 256 devices: a whole 4x4x8 slice. The times are simulated.
256 devices in a mesh: seq: 128 (over x, y, z), resp: 2 (over core).
Axes of the slice: x: 4, y: 4, z: 8, core: 2. Of those that a mesh axis runs over, the one named last changes fastest.
Arguments:
- cat_query: bfloat16 [16384, 4096], P('seq', 'resp'), may hold values from -6 to 6
- cat_key: bfloat16 [16384, 4096], P('seq', 'resp'), may hold values from -6 to 6
- cat_value: bfloat16 [16384, 4096], P('seq', 'resp'), may hold values from -6 to 6
- resp_query: bfloat16 [32768, 4096], P(('seq', 'resp')), may hold values from -6 to 6
- resp_key: bfloat16 [32768, 4096], P(('seq', 'resp')), may hold values from -6 to 6
- resp_value: bfloat16 [32768, 4096], P(('seq', 'resp')), may hold values from -6 to 6
- resp_lengths: int32 [256, 3], P(('seq', 'resp')), may hold values from 1 to 64, 128 in all within a row
- norm_gain: float32 [4096], replicated, may hold values from 0.1 to 1.9
Outputs:
- cat_out: bfloat16 [16384, 4096], P('seq', 'resp')
- resp_out: bfloat16 [32768, 4096], P(('seq', 'resp'))
Inputs may be any that keep to these rules, and one draw needn't show every extreme that they name: `resp_lengths`: each row's 3 lengths sum to 128.
All inputs are finite; a program needn't handle non-finite values.
Results may differ from a plain program's by a relative error of at most 0.0021.
Values sent between devices are 32-bit elements; how exact they have to be, the bound alone decides.
A program may use at most 320 MiB of HBM per device.

v0:
```python
import jax
import jax.numpy as jnp
from jax import lax
from jax.sharding import PartitionSpec as P

DH = 128


def entering(value, axis, combine, identity):
    peers, here = (lax.axis_size(axis), lax.axis_index(axis))
    everything = lax.all_gather(value, axis)
    start = jnp.broadcast_to(jnp.asarray(identity, value.dtype), value.shape)

    def lap(k, before):
        reached = k < here
        new = combine(before, everything[k])
        return jnp.where(reached, new, before)

    return lax.fori_loop(0, peers, lap, start)


def attend(query, key, value, mask, state, heads):
    rows = query.shape[0]
    qh = query.reshape(rows, heads, DH)
    kh = key.reshape(rows, heads, DH)
    vh = value.reshape(rows, heads, DH)
    scores = jnp.einsum("thd,shd->hts", qh, kh, preferred_element_type=jnp.float32)
    scores = jnp.where(mask[None, :, :], scores, 0.0).astype(jnp.bfloat16)
    inner = jnp.einsum("hts,shd->thd", scores, vh, preferred_element_type=jnp.float32)
    outer = jnp.einsum(
        "thd,hde->the", qh.astype(jnp.float32), state, precision=lax.Precision.HIGHEST
    )
    return inner + outer


def block_state(key, value, heads):
    rows = key.shape[0]
    kh = key.reshape(rows, heads, DH)
    vh = value.reshape(rows, heads, DH)
    return jnp.einsum("shd,she->hde", kh, vh, preferred_element_type=jnp.float32)


def head_norm(raw, gain, heads):
    square = jnp.mean(raw * raw, axis=-1, keepdims=True)
    scaled = raw * lax.rsqrt(square + 1e-06) * gain.reshape(heads, DH)
    return scaled.reshape(raw.shape[0], heads * DH).astype(jnp.bfloat16)


def add_states(earlier, later):
    return earlier + later


def per_device(
    cat_query, cat_key, cat_value, resp_query, resp_key, resp_value, resp_lengths, norm_gain
):
    heads_here = cat_query.shape[1] // DH
    all_heads = resp_query.shape[1] // DH
    local_state = block_state(cat_key, cat_value, heads_here)
    prefix = entering(local_state, "seq", add_states, jnp.zeros_like(local_state))
    places = jnp.arange(cat_query.shape[0], dtype=jnp.int32)
    causal = places[None, :] <= places[:, None]
    cat_raw = attend(cat_query, cat_key, cat_value, causal, prefix, heads_here)
    offset = lax.axis_index("resp") * (heads_here * DH)
    cat_gain = lax.dynamic_slice_in_dim(norm_gain, offset, heads_here * DH)
    cat_out = head_norm(cat_raw, cat_gain, heads_here)
    total = lax.psum(local_state, "seq")
    whole = lax.all_gather(total, "resp", axis=0, tiled=True)
    rows = jnp.arange(resp_query.shape[0], dtype=jnp.int32)
    ends = jnp.cumsum(resp_lengths[0])
    segment = jnp.sum((rows[:, None] >= ends[None, :]).astype(jnp.int32), axis=1)
    mask = (segment[:, None] == segment[None, :]) & (rows[None, :] <= rows[:, None])
    resp_raw = attend(resp_query, resp_key, resp_value, mask, whole, all_heads)
    resp_out = head_norm(resp_raw, norm_gain, all_heads)
    return (cat_out, resp_out)


def solution(mesh):
    placed = (
        P("seq", "resp"),
        P("seq", "resp"),
        P("seq", "resp"),
        P(("seq", "resp"), None),
        P(("seq", "resp"), None),
        P(("seq", "resp"), None),
        P(("seq", "resp"), None),
        P(),
    )
    return jax.shard_map(
        per_device,
        mesh=mesh,
        in_specs=placed,
        out_specs=(P("seq", "resp"), P(("seq", "resp"), None)),
        check_vma=False,
    )
```

profile of v0, /device:TPU:1, one launch (start us, length us, event | category | flops | bytes accessed | tf_op | source)
XLA Modules:
  0.0 1071.7 jit_solution(10842550589491584240)
XLA Ops:
  8.6 2.3 fusion.16
  11.0 611.6 %all-gather.6.cloned.1.call-done = f32[2048,128,128]{2,1,0:T(8,128)} async-done(((f32[16,128,128]{2,1,0:T(8,128)}), f32[2048,128,128]{2,1,0:T(8,128)}) %all-gather.6.cloned.1.call-update) | async-done | bytes 134217744 | tf_op jit(solution)/shard_map/all_gather | solution.py:11
  623.4 2.3 copy.46
  626.0 4.5 fusion
  630.5 212.7 %all-reduce.2.cloned.1.call-done = f32[16,128,128]{2,1,0:T(8,128)} async-done(((f32[16,128,128]{2,1,0:T(8,128)}), f32[16,128,128]{2,1,0:T(8,128)}) %all-reduce.2.cloned.1.call-update) | async-done | bytes 1048592 | tf_op jit(solution)/shard_map/psum | solution.py:66
  843.2 206.9 %while.14 = (s32[]{:T(128)}, f32[16,128,128]{2,1,0:T(8,128)S(1)}, s32[]{:T(128)}, f32[128,16,128,128]{3,2,1,0:T(8,128)}, s32[]{:T(128)}, /*index=5*/s32[]{:T(128)}) while((s32[]{:T(128)}, f32[16,128,128]{2,1,0:T(8,128)S(1)}, s32[]{:T(128)}, f32[128,16,128,128]{3,2,1,0:T(8,128)}, s32[]{:T(128)}, /*index=5*/s32[]{:T(128)}) %tuple.41), condition=%wide.region_1.2_spmd.clone, body=%wide.region_0.1_spmd.clone.sunk | while | flops 786436 | bytes 3145829 | solution.py:19
  843.2 1.6 add_select_fusion.2
  844.9 1.6 add_select_fusion.2
  848.1 1.6 add_select_fusion.2
  851.4 1.6 add_select_fusion.2
  854.6 1.6 add_select_fusion.2
  857.8 1.7 add_select_fusion.2
  859.5 1.7 add_select_fusion.2
  861.2 1.6 add_select_fusion.2
  862.9 1.6 add_select_fusion.2
  864.5 1.6 add_select_fusion.2
  867.7 1.6 add_select_fusion.2
  870.9 1.6 add_select_fusion.2
  874.2 1.6 add_select_fusion.2
  877.4 1.6 add_select_fusion.2
  880.6 1.6 add_select_fusion.2
  883.8 1.6 add_select_fusion.2
  885.5 1.6 add_select_fusion.2
  887.1 1.6 add_select_fusion.2
  888.7 1.6 add_select_fusion.2
  890.3 1.6 add_select_fusion.2
  891.9 1.6 add_select_fusion.2
  893.5 1.6 add_select_fusion.2
  895.1 1.6 add_select_fusion.2
  898.4 1.6 add_select_fusion.2
  901.6 1.6 add_select_fusion.2
  904.8 1.6 add_select_fusion.2
  908.1 1.6 add_select_fusion.2
  911.3 1.6 add_select_fusion.2
  914.5 1.6 add_select_fusion.2
  916.1 1.6 add_select_fusion.2
  917.7 1.6 add_select_fusion.2
  919.4 1.6 add_select_fusion.2
  921.0 1.6 add_select_fusion.2
  922.6 1.6 add_select_fusion.2
  924.2 1.6 add_select_fusion.2
  925.8 1.6 add_select_fusion.2
  929.0 1.6 add_select_fusion.2
  932.3 1.6 add_select_fusion.2
  935.5 1.6 add_select_fusion.2
  938.7 1.6 add_select_fusion.2
  942.0 1.6 add_select_fusion.2
  945.2 1.6 add_select_fusion.2
  946.8 1.6 add_select_fusion.2
  948.4 1.6 add_select_fusion.2
  950.0 1.6 add_select_fusion.2
  951.6 1.6 add_select_fusion.2
  953.3 1.6 add_select_fusion.2
  954.9 1.6 add_select_fusion.2
  956.5 1.6 add_select_fusion.2
  959.7 1.6 add_select_fusion.2
  962.9 1.6 add_select_fusion.2
  966.2 1.6 add_select_fusion.2
  969.4 1.6 add_select_fusion.2
  1050.1 2.0 convolution_bitcast_fusion.1
  1052.1 3.0 multiply_reduce_fusion.1
  1055.1 2.5 multiply_convert_fusion.1
  1057.6 2.0 copy.42
  1059.7 3.5 multiply_reduce_fusion
  (103 shorter events, 123.9 us)
Async XLA Ops:
  7.2 618.9 %copy-start = (bf16[128,4096]{1,0:T(8,128)(2,1)S(1)}, bf16[128,4096]{1,0:T(8,128)(2,1)}, u32[]{:S(2)}) copy-start(bf16[128,4096]{1,0:T(8,128)(2,1)} %param.13) | copy-start | bytes 3145732
  7.2 615.4 %all-gather.6.cloned.1.call-start = ((), (), s32[]{:S(2)}) async-start(), calls=%async_computation.2 | async-start | bytes 135266304 | tf_op jit(solution)/shard_map/all_gather | solution.py:11
  10.9 614.7 %copy-start.4 = (s32[1,3]{1,0:T(1,128)S(1)}, s32[1,3]{1,0:T(1,128)}, u32[]{:S(2)}) copy-start(s32[1,3]{1,0:T(1,128)} %param.16) | copy-start | bytes 40
  10.9 614.9 %copy-start.3 = (f32[4096]{0:T(1024)S(1)}, f32[4096]{0:T(1024)}, u32[]{:S(2)}) copy-start(f32[4096]{0:T(1024)} %param.17) | copy-start | bytes 49156
  622.6 220.6 %all-reduce.2.cloned.1.call-start = ((), (), s32[]{:S(2)}) async-start(), calls=%async_computation | async-start | bytes 2097152 | tf_op jit(solution)/shard_map/psum | solution.py:66
  623.3 436.4 %all-gather.4.cloned.1.call-start = ((), (), s32[]{:S(2)}) async-start(), calls=%async_computation.1 | async-start | bytes 3145728 | tf_op jit(solution)/shard_map/all_gather | solution.py:67
  843.2 206.9 %copy-start.2 = (bf16[128,2048]{1,0:T(8,128)(2,1)S(1)}, bf16[128,2048]{1,0:T(8,128)(2,1)}, u32[]{:S(2)}) copy-start(bf16[128,2048]{1,0:T(8,128)(2,1)} %param.10) | copy-start | bytes 1572868
  1055.1 4.6 copy-start.1
Sparse Core Ops, SparseCore 0:
  12.2 610.2 all-gather.5
  629.3 213.8 all-reduce.1
  845.0 18.5 all-gather.3
where the time goes:
time: 1080 us; the launch traced here: 1070 us
  waiting for transfers between devices  825 us (76%)
  other arithmetic  207 us (19%)
  matrix products  15.3 us (1%)
  between operations  13.8 us (1%)
    all_gather x1, waiting for transfers between devices, entering(): everything = lax.all_gather(value, axis)  612 us
    psum x1, waiting for transfers between devices, per_device(): total = lax.psum(local_state, 'seq')  213 us
    select_n x128, other arithmetic, lap(): return jnp.where(reached, new, before)  204 us
  transfers between devices with their start and end apart: 3, of which 2 were waited for; matrix products, arithmetic and copies ran while one was open for 21% of the time, Pallas kernels for 0%

commit v1 on v0

v1 whole, which is shorter than its diff:
```python
import jax
import jax.numpy as jnp
from jax import lax
from jax.sharding import PartitionSpec as P

DH = 128


def attend_inner(query, key, value, mask, heads):
    rows = query.shape[0]
    qh = query.reshape(rows, heads, DH)
    kh = key.reshape(rows, heads, DH)
    vh = value.reshape(rows, heads, DH)
    scores = jnp.einsum("thd,shd->hts", qh, kh, preferred_element_type=jnp.float32)
    scores = jnp.where(mask[None, :, :], scores, 0.0).astype(jnp.bfloat16)
    return jnp.einsum("hts,shd->thd", scores, vh, preferred_element_type=jnp.float32)


def attend_outer(query, state, heads):
    rows = query.shape[0]
    qh = query.reshape(rows, heads, DH).astype(jnp.float32)
    return jnp.einsum("thd,hde->the", qh, state, precision=lax.Precision.HIGHEST)


def block_state(key, value, heads):
    rows = key.shape[0]
    kh = key.reshape(rows, heads, DH)
    vh = value.reshape(rows, heads, DH)
    return jnp.einsum("shd,she->hde", kh, vh, preferred_element_type=jnp.float32)


def head_norm(raw, gain, heads):
    square = jnp.mean(raw * raw, axis=-1, keepdims=True)
    scaled = raw * lax.rsqrt(square + 1e-06) * gain.reshape(heads, DH)
    return scaled.reshape(raw.shape[0], heads * DH).astype(jnp.bfloat16)


def transpose_scan(local_state):
    peers = lax.axis_size("seq")
    chunks = local_state.reshape(peers, -1, DH)
    gathered = lax.all_to_all(chunks, "seq", 0, 0, tiled=True)
    inclusive = jnp.cumsum(gathered, axis=0)
    exclusive = jnp.concatenate([jnp.zeros_like(inclusive[:1]), inclusive[:-1]], axis=0)
    prefix = lax.all_to_all(exclusive, "seq", 0, 0, tiled=True)
    return prefix.reshape(local_state.shape), inclusive[-1]


def per_device(
    cat_query, cat_key, cat_value, resp_query, resp_key, resp_value, resp_lengths, norm_gain
):
    heads_here = cat_query.shape[1] // DH
    all_heads = resp_query.shape[1] // DH
    local_state = block_state(cat_key, cat_value, heads_here)
    prefix, total_chunk = transpose_scan(local_state)
    whole = lax.all_gather(total_chunk, ("resp", "seq"), axis=0, tiled=True)
    whole = whole.reshape(all_heads, DH, DH)

    places = jnp.arange(cat_query.shape[0], dtype=jnp.int32)
    causal = places[None, :] <= places[:, None]
    cat_inner = attend_inner(cat_query, cat_key, cat_value, causal, heads_here)
    rows = jnp.arange(resp_query.shape[0], dtype=jnp.int32)
    ends = jnp.cumsum(resp_lengths[0])
    segment = jnp.sum((rows[:, None] >= ends[None, :]).astype(jnp.int32), axis=1)
    mask = (segment[:, None] == segment[None, :]) & (rows[None, :] <= rows[:, None])
    resp_inner = attend_inner(resp_query, resp_key, resp_value, mask, all_heads)

    cat_raw = cat_inner + attend_outer(cat_query, prefix, heads_here)
    offset = lax.axis_index("resp") * (heads_here * DH)
    cat_gain = lax.dynamic_slice_in_dim(norm_gain, offset, heads_here * DH)
    cat_out = head_norm(cat_raw, cat_gain, heads_here)
    resp_raw = resp_inner + attend_outer(resp_query, whole, all_heads)
    resp_out = head_norm(resp_raw, norm_gain, all_heads)
    return (cat_out, resp_out)


def solution(mesh):
    placed = (
        P("seq", "resp"),
        P("seq", "resp"),
        P("seq", "resp"),
        P(("seq", "resp"), None),
        P(("seq", "resp"), None),
        P(("seq", "resp"), None),
        P(("seq", "resp"), None),
        P(),
    )
    return jax.shard_map(
        per_device,
        mesh=mesh,
        in_specs=placed,
        out_specs=(P("seq", "resp"), P(("seq", "resp"), None)),
        check_vma=False,
    )
```

time: 1080 us -> 195 us (0.18)
  waiting for transfers between devices: 825 us -> 76.9 us
  other arithmetic: 207 us -> 26.7 us
  blocking collectives: 0 us -> 46.4 us
    all_gather x2 -> x1, waiting for transfers between devices: 612 us -> 53.5 us  [per_device(): whole = lax.all_gather(total_chunk, ('resp', 'seq'), axis=0, tiled=True)]
    psum x1 -> x0, waiting for transfers between devices: 213 us -> none  [per_device(): total = lax.psum(local_state, 'seq')]
    select_n x128 -> x0, other arithmetic: 204 us -> none  [lap(): return jnp.where(reached, new, before)]
    all_to_all x0 -> x1, blocking collectives: none -> 46.4 us  [transpose_scan(): gathered = lax.all_to_all(chunks, 'seq', 0, 0, tiled=True)]
    all_to_all x0 -> x1, waiting for transfers between devices: none -> 23.4 us  [transpose_scan(): prefix = lax.all_to_all(exclusive, 'seq', 0, 0, tiled=True)]
    another operation x1 -> x2, other arithmetic: 0.18 us -> 23.4 us  [the longest x1 23.2 us: transpose_scan(): inclusive = jnp.cumsum(gathered, axis=0)]
  transfers between devices with their start and end apart: 3 -> 2, of which waited for: 2 -> 2; matrix products, arithmetic and copies ran while one was open for 21% -> 9% of each run, Pallas kernels for 0% -> 0%
where the time goes in v1:
time: 195 us; the launch traced here: 194 us
  waiting for transfers between devices  76.9 us (39%)
  blocking collectives  46.4 us (24%)
  other arithmetic  26.7 us (14%)
  matrix products  14.8 us (8%)
  between operations  14.1 us (7%)
  local copies, waits for them, and re-layouts  7.8 us (4%)
  starting transfers between devices  7.49 us (4%)
    all_gather x1, waiting for transfers between devices, per_device(): whole = lax.all_gather(total_chunk, ('resp', 'seq'), axis=0, tiled=True)  53.5 us
    all_to_all x1, blocking collectives, transpose_scan(): gathered = lax.all_to_all(chunks, 'seq', 0, 0, tiled=True)  46.4 us
    all_to_all x1, waiting for transfers between devices, transpose_scan(): prefix = lax.all_to_all(exclusive, 'seq', 0, 0, tiled=True)  23.4 us
    another operation x1, other arithmetic, transpose_scan(): inclusive = jnp.cumsum(gathered, axis=0)  23.2 us
    all_to_all x1, starting transfers between devices, transpose_scan(): prefix = lax.all_to_all(exclusive, 'seq', 0, 0, tiled=True)  7.45 us
    dot_general x2, matrix products, attend_outer(): jnp.einsum('thd,hde->the', qh, state, precision=lax.Precision.HIGHEST)  6.82 us
    dot_general x2, matrix products, attend_inner(): jnp.einsum('hts,shd->thd', scores, vh, preferred_element_type=jnp.float32)  6.45 us
  transfers between devices with their start and end apart: 2, of which 2 were waited for; matrix products, arithmetic and copies ran while one was open for 9% of the time, Pallas kernels for 0%

profile of v1, /device:TPU:1, one launch (start us, length us, event | category | flops | bytes accessed | tf_op | source)
XLA Modules:
  0.0 194.2 jit_solution(13972053392642024056)
XLA Ops:
  7.2 0.0 copy-start
  7.2 0.0 all-gather.3.cloned.1.call-start
  7.2 1.4 copy.45
  8.6 0.0 copy-start.1
  8.6 1.5 fusion.16
  10.2 46.4 %all_to_all.10 = f32[128,16,128]{2,1,0:T(8,128)S(1)} all-to-all(f32[128,16,128]{2,1,0:T(8,128)S(1)} %bitcast.87), channel_id=1, replica_groups=mesh['seq'=128,'resp'=2] {'seq'}, dimensions={0} | all-to-all | bytes 2097152 | tf_op jit(solution)/shard_map/all_to_all | solution.py:41
  56.5 0.0 copy-done.1
  56.5 23.2 %fusion.32 = f32[128,16,128]{2,1,0:T(8,128)S(1)} fusion(f32[128,16,128]{2,1,0:T(8,128)S(1)} %all_to_all.10), kind=kOutput, calls=%fused_computation.40 | output fusion | flops 33292288 | bytes 2097152 | tf_op jit(solution)/shard_map/jit(cumsum)/reduce_window_sum | solution.py:42
  79.8 0.6 slice.9
  80.4 0.0 all-gather.3.cloned.1.call-update
  80.4 0.1 slice.8
  80.5 0.0 copy-start.4
  80.5 0.0 copy-start.2
  80.5 1.0 concatenate.3
  81.6 0.0 copy-start.3
  81.6 7.4 %all-to-all-start.1 = ((f32[128,16,128]{2,1,0:T(8,128)}), f32[128,16,128]{2,1,0:T(8,128)}, u32[]{:S(2)}, u32[]{:S(2)}) async-start(f32[128,16,128]{2,1,0:T(8,128)} %concatenate.3), calls=%async_computation.1 | async-start | bytes 2097152 | tf_op jit(solution)/shard_map/all_to_all | solution.py:44
  89.0 0.0 copy-done.4
  89.0 0.2 reduce-window.8
  89.2 0.0 copy-done.2
  89.2 1.3 copy.44
  90.5 0.0 copy-done.3
  90.5 0.1 convert_reduce_fusion
  90.6 0.1 compare_and_fusion
  90.7 0.0 copy-done
  90.7 3.1 %fusion = f32[32,128,128]{1,2,0:T(8,128)S(1)} fusion(bf16[128,32,128]{0,2,1:T(8,128)(2,1)} %bitcast.85, pred[128,128]{1,0:T(8,128)(4,1)S(1)} %compare_and_fusion, bf16[128,4096]{1,0:T(8,128)(2,1)} %param.12, bf16[128,4096]{1,0:T(8,128)(2,1)S(1)} %copy-done), kind=kOutput, calls=%fused_computation.5 | convolution fusion | flops 269484032 | bytes 5259264 | tf_op jit(solution)/shard_map/hts,shd->thd/dot_general | solution.py:16
  93.9 23.4 %all-to-all-done.1 = f32[128,16,128]{2,1,0:T(8,128)} async-done(((f32[128,16,128]{2,1,0:T(8,128)}), f32[128,16,128]{2,1,0:T(8,128)}, u32[]{:S(2)}, u32[]{:S(2)}) %all-to-all-start.1) | async-done | bytes 1048608 | tf_op jit(solution)/shard_map/all_to_all | solution.py:44
  117.3 3.3 %convolution_bitcast_fusion.1 = f32[128,16,128]{0,2,1:T(8,128)} fusion(f32[16,128,128]{2,1,0:T(8,128)} %bitcast.2, bf16[128,2048]{1,0:T(8,128)(2,1)} %param.8), kind=kOutput, calls=%fused_computation.8 | convolution fusion | flops 402653184 | bytes 2621440 | tf_op jit(solution)/shard_map/thd,hde->the/dot_general | solution.py:22
  120.6 3.3 %multiply_reduce_fusion.1 = (f32[128,16]{0,1:T(8,128)S(1)}, f32[128,16,128]{0,2,1:T(8,128)}) fusion(f32[128,16,128]{0,2,1:T(8,128)} %convolution_bitcast_fusion.1, bf16[128,16,128]{0,2,1:T(8,128)(2,1)} %bitcast.84, pred[128,128]{1,0:T(8,128)(4,1)S(1)} %iota_compare_fusion, bf16[128,2048]{1,0:T(8,128)(2,1)} %param.10, bf16[128,2048]{1,0:T(8,128)(2,1)} %param.8), kind=kOutput, calls=%fused_computation.16 | convolution fusion | flops 135526400 | bytes 3694592 | tf_op jit(solution)/shard_map/hts,shd->thd/dot_general | solution.py:16
  123.9 2.4 %multiply_convert_fusion.1 = bf16[128,16,128]{0,2,1:T(8,128)(2,1)} fusion(f32[128,16,128]{0,2,1:T(8,128)} %get-tuple-element.9, f32[16,128]{1,0:T(8,128)S(1)} %dynamic-slice_bitcast_fusion, f32[128,16]{0,1:T(8,128)S(1)} %add_rsqrt_fusion.1), kind=kLoop, calls=%fused_computation.15 | loop fusion | flops 786432 | bytes 1589248 | tf_op jit(solution)/shard_map/convert_element_type | solution.py:35
  126.3 2.0 %copy.40 = bf16[128,2048]{1,0:T(8,128)(2,1)} copy(bf16[128,2048]{0,1:T(8,128)(2,1)} %bitcast.89) | data formatting | bytes 1048576
  128.3 53.5 %all-gather.3.cloned.1.call-done = f32[1,4096,128]{2,1,0:T(8,128)} async-done(((f32[1,16,128]{2,1,0:T(8,128)}), f32[1,4096,128]{2,1,0:T(8,128)}) %all-gather.3.cloned.1.call-update) | async-done | bytes 2097168 | tf_op jit(solution)/shard_map/all_gather | solution.py:55
  181.8 3.5 %multiply_reduce_fusion = (f32[128,32]{0,1:T(8,128)S(1)}, f32[128,32,128]{0,2,1:T(8,128)S(1)}) fusion(f32[32,128,128]{2,1,0:T(8,128)} %bitcast.88, f32[32,128,128]{1,2,0:T(8,128)S(1)} %fusion, bf16[128,4096]{1,0:T(8,128)(2,1)S(1)} %copy-done), kind=kOutput, calls=%fused_computation.2 | convolution fusion | flops 806875136 | bytes 7356416 | tf_op jit(solution)/shard_map/thd,hde->the/dot_general | solution.py:22
  185.3 0.7 multiply_convert_fusion
  186.1 1.3 copy.41
  (4 shorter events, 0.0 us)
Async XLA Ops:
  7.2 83.6 %copy-start = (bf16[128,4096]{1,0:T(8,128)(2,1)S(1)}, bf16[128,4096]{1,0:T(8,128)(2,1)}, u32[]{:S(2)}) copy-start(bf16[128,4096]{1,0:T(8,128)(2,1)} %param.11) | copy-start | bytes 3145732
  7.2 174.7 %all-gather.3.cloned.1.call-start = ((), (), s32[]{:S(2)}) async-start(), calls=%async_computation.2 | async-start | bytes 2105344 | tf_op jit(solution)/shard_map/all_gather | solution.py:55
  8.6 47.9 %copy-start.1 = (bf16[128,2048]{0,1:T(8,128)(2,1)}, bf16[128,2048]{0,1:T(8,128)(2,1)S(1)}, u32[]{:S(2)}) copy-start(bf16[128,2048]{0,1:T(8,128)(2,1)S(1)} %copy.45) | copy-start | bytes 1572868
  80.5 8.5 %copy-start.4 = (s32[1,3]{1,0:T(1,128)S(1)}, s32[1,3]{1,0:T(1,128)}, u32[]{:S(2)}) copy-start(s32[1,3]{1,0:T(1,128)} %param.14) | copy-start | bytes 40
  80.5 8.7 %copy-start.2 = (bf16[128,4096]{1,0:T(8,128)(2,1)S(1)}, bf16[128,4096]{1,0:T(8,128)(2,1)}, u32[]{:S(2)}) copy-start(bf16[128,4096]{1,0:T(8,128)(2,1)} %param.13) | copy-start | bytes 3145732
  81.6 9.0 %copy-start.3 = (f32[4096]{0:T(1024)S(1)}, f32[4096]{0:T(1024)}, u32[]{:S(2)}) copy-start(f32[4096]{0:T(1024)} %param.15) | copy-start | bytes 49156
  81.6 35.7 %all-to-all-start.1 = ((f32[128,16,128]{2,1,0:T(8,128)}), f32[128,16,128]{2,1,0:T(8,128)}, u32[]{:S(2)}, u32[]{:S(2)}) async-start(f32[128,16,128]{2,1,0:T(8,128)} %concatenate.3), calls=%async_computation.1 | async-start | bytes 2097152 | tf_op jit(solution)/shard_map/all_to_all | solution.py:44
Sparse Core Ops, SparseCore 0:
  80.5 101.2 all-gather.2

commit v2 on v1

--- a/solution.py
+++ b/solution.py
@@ -39,10 +39,15 @@
     peers = lax.axis_size("seq")
     chunks = local_state.reshape(peers, -1, DH)
     gathered = lax.all_to_all(chunks, "seq", 0, 0, tiled=True)
-    inclusive = jnp.cumsum(gathered, axis=0)
-    exclusive = jnp.concatenate([jnp.zeros_like(inclusive[:1]), inclusive[:-1]], axis=0)
+    before = lax.broadcasted_iota(jnp.int32, (peers, peers), 1) < lax.broadcasted_iota(
+        jnp.int32, (peers, peers), 0
+    )
+    flat = gathered.reshape(peers, -1)
+    exclusive = jnp.dot(
+        before.astype(jnp.float32), flat, precision=lax.Precision.HIGHEST
+    ).reshape(chunks.shape)
     prefix = lax.all_to_all(exclusive, "seq", 0, 0, tiled=True)
-    return prefix.reshape(local_state.shape), inclusive[-1]
+    return prefix.reshape(local_state.shape)
 
 
 def per_device(
@@ -51,9 +56,9 @@
     heads_here = cat_query.shape[1] // DH
     all_heads = resp_query.shape[1] // DH
     local_state = block_state(cat_key, cat_value, heads_here)
-    prefix, total_chunk = transpose_scan(local_state)
-    whole = lax.all_gather(total_chunk, ("resp", "seq"), axis=0, tiled=True)
-    whole = whole.reshape(all_heads, DH, DH)
+    total = lax.psum(local_state, "seq")
+    prefix = transpose_scan(local_state)
+    whole = lax.all_gather(total, "resp", axis=0, tiled=True)
 
     places = jnp.arange(cat_query.shape[0], dtype=jnp.int32)
     causal = places[None, :] <= places[:, None]

time: 195 us -> 309 us (1.58); the launches traced: 194 us -> 304 us
  waiting for transfers between devices: 76.9 us -> 239 us
  blocking collectives: 46.4 us -> 0 us
  other arithmetic: 26.7 us -> 1.44 us
  starting transfers between devices: 7.49 us -> 27.4 us
    psum x0 -> x1, waiting for transfers between devices: none -> 224 us  [per_device(): total = lax.psum(local_state, 'seq')]
    all_gather x1, waiting for transfers between devices: 53.5 us -> 1.62 us  [per_device(): whole = lax.all_gather(total, 'resp', axis=0, tiled=True)]
    all_to_all x1 -> x0, blocking collectives: 46.4 us -> none  [transpose_scan(): gathered = lax.all_to_all(chunks, 'seq', 0, 0, tiled=True)]
    another operation x2 -> x1, other arithmetic: 23.4 us -> 0.18 us  [the longest x1 23.2 us: transpose_scan(): inclusive = jnp.cumsum(gathered, axis=0)]
    all_to_all x0 -> x1, starting transfers between devices: none -> 16.3 us  [transpose_scan(): gathered = lax.all_to_all(chunks, 'seq', 0, 0, tiled=True)]
    all_to_all x1, waiting for transfers between devices: 23.4 us -> 13.1 us  [transpose_scan(): prefix = lax.all_to_all(exclusive, 'seq', 0, 0, tiled=True)]
    all_to_all x1, starting transfers between devices: 7.45 us -> 10.9 us  [transpose_scan(): prefix = lax.all_to_all(exclusive, 'seq', 0, 0, tiled=True)]
  transfers between devices with their start and end apart: 2 -> 4, of which waited for: 2 -> 3; matrix products, arithmetic and copies ran while one was open for 9% -> 4% of each run, Pallas kernels for 0% -> 0%
where the time goes in v2:
time: 309 us; the launch traced here: 304 us
  waiting for transfers between devices  239 us (77%)
  starting transfers between devices  27.4 us (9%)
  matrix products  15.3 us (5%)
  between operations  14.2 us (5%)
  local copies, waits for them, and re-layouts  7.08 us (2%)
    psum x1, waiting for transfers between devices, per_device(): total = lax.psum(local_state, 'seq')  224 us
    all_to_all x1, starting transfers between devices, transpose_scan(): gathered = lax.all_to_all(chunks, 'seq', 0, 0, tiled=True)  16.3 us
    all_to_all x1, waiting for transfers between devices, transpose_scan(): prefix = lax.all_to_all(exclusive, 'seq', 0, 0, tiled=True)  13.1 us
    all_to_all x1, starting transfers between devices, transpose_scan(): prefix = lax.all_to_all(exclusive, 'seq', 0, 0, tiled=True)  10.9 us
    dot_general x2, matrix products, attend_outer(): jnp.einsum('thd,hde->the', qh, state, precision=lax.Precision.HIGHEST)  6.68 us
  transfers between devices with their start and end apart: 4, of which 3 were waited for; matrix products, arithmetic and copies ran while one was open for 4% of the time, Pallas kernels for 0%

profile of v2, /device:TPU:1, one launch (start us, length us, event | category | flops | bytes accessed | tf_op | source)
XLA Modules:
  0.0 304.3 jit_solution(7206592568741554956)
XLA Ops:
  7.2 0.0 copy-start
  7.2 1.4 copy.68
  8.6 0.0 copy-start.1
  8.6 2.5 fusion.18
  11.1 0.0 copy-done.1
  11.1 16.3 %all-to-all-start = ((f32[128,16,128]{2,1,0:T(8,128)}), f32[128,16,128]{2,1,0:T(8,128)S(1)}, u32[]{:S(2)}, u32[]{:S(2)}) async-start(f32[128,16,128]{2,1,0:T(8,128)} %bitcast.2), calls=%async_computation | async-start | bytes 2097152 | tf_op jit(solution)/shard_map/all_to_all | solution.py:41
  27.4 0.0 all-reduce.2.cloned.1.call-start
  27.5 0.7 all-reduce.2.cloned.1.call-update
  28.2 0.0 all-gather.2.cloned.1.call-start
  28.2 223.5 %all-reduce.2.cloned.1.call-done = f32[16,128,128]{2,1,0:T(8,128)} async-done(((f32[16,128,128]{2,1,0:T(8,128)}), f32[16,128,128]{2,1,0:T(8,128)}) %all-reduce.2.cloned.1.call-update) | async-done | bytes 1048592 | tf_op jit(solution)/shard_map/psum | solution.py:59
  251.8 0.0 all-gather.2.cloned.1.call-update
  251.8 0.0 all-to-all-done
  251.8 0.4 copy.66
  252.2 0.7 fusion.10
  252.9 0.0 copy-start.6
  252.9 0.0 copy-start.4
  252.9 1.6 copy.54
  254.5 0.0 copy-start.5
  254.5 10.9 %all-to-all-start.1 = ((f32[128,16,128]{2,1,0:T(8,128)}), f32[128,16,128]{2,1,0:T(8,128)}, u32[]{:S(2)}, u32[]{:S(2)}) async-start(f32[128,16,128]{2,1,0:T(8,128)} %copy.54), calls=%async_computation.1 | async-start | bytes 2097152 | tf_op jit(solution)/shard_map/all_to_all | solution.py:49
  265.5 0.0 copy-done.6
  265.5 0.2 reduce-window.8
  265.7 0.0 copy-done.4
  265.7 1.3 copy.67
  267.0 0.0 copy-done.5
  267.0 0.1 convert_reduce_fusion
  267.1 0.1 compare_and_fusion
  267.2 0.0 copy-done
  267.2 3.3 %fusion = f32[32,128,128]{1,2,0:T(8,128)S(1)} fusion(bf16[128,32,128]{0,2,1:T(8,128)(2,1)} %bitcast.93, pred[128,128]{1,0:T(8,128)(4,1)S(1)} %compare_and_fusion, bf16[128,4096]{1,0:T(8,128)(2,1)} %param.12, bf16[128,4096]{1,0:T(8,128)(2,1)S(1)} %copy-done), kind=kOutput, calls=%fused_computation.5 | convolution fusion | flops 269484032 | bytes 5259264 | tf_op jit(solution)/shard_map/hts,shd->thd/dot_general | solution.py:16
  270.5 1.6 all-gather.2.cloned.1.call-done
  272.1 3.5 %multiply_reduce_fusion = (f32[128,32]{0,1:T(8,128)S(1)}, f32[128,32,128]{0,2,1:T(8,128)S(1)}) fusion(f32[32,128,128]{2,1,0:T(8,128)} %all-gather.2.cloned.1.call-done, f32[32,128,128]{1,2,0:T(8,128)S(1)} %fusion, bf16[128,4096]{1,0:T(8,128)(2,1)S(1)} %copy-done), kind=kOutput, calls=%fused_computation.2 | convolution fusion | flops 806875136 | bytes 7356416 | tf_op jit(solution)/shard_map/thd,hde->the/dot_general | solution.py:22
  275.7 0.0 copy-start.3
  275.7 0.7 multiply_convert_fusion
  276.4 0.0 copy-start.2
  276.4 1.3 copy.63
  277.7 13.1 %all-to-all-done.1 = f32[128,16,128]{2,1,0:T(8,128)} async-done(((f32[128,16,128]{2,1,0:T(8,128)}), f32[128,16,128]{2,1,0:T(8,128)}, u32[]{:S(2)}, u32[]{:S(2)}) %all-to-all-start.1) | async-done | bytes 1048608 | tf_op jit(solution)/shard_map/all_to_all | solution.py:49
  290.8 0.0 copy-done.3
  290.8 3.2 %convolution_bitcast_fusion.1 = f32[128,16,128]{0,2,1:T(8,128)} fusion(f32[16,128,128]{2,1,0:T(8,128)} %bitcast.6, bf16[128,2048]{1,0:T(8,128)(2,1)S(1)} %copy-done.3), kind=kOutput, calls=%fused_computation.8 | convolution fusion | flops 402653184 | bytes 2621440 | tf_op jit(solution)/shard_map/thd,hde->the/dot_general | solution.py:22
  294.0 0.0 copy-done.2
  294.0 2.1 multiply_reduce_fusion.1
  296.1 0.3 multiply_convert_fusion.1
  296.5 1.0 copy.62
  (4 shorter events, 0.0 us)
Async XLA Ops:
  7.2 260.0 %copy-start = (bf16[128,4096]{1,0:T(8,128)(2,1)S(1)}, bf16[128,4096]{1,0:T(8,128)(2,1)}, u32[]{:S(2)}) copy-start(bf16[128,4096]{1,0:T(8,128)(2,1)} %param.11) | copy-start | bytes 3145732
  8.6 2.5 copy-start.1
  11.1 240.7 %all-to-all-start = ((f32[128,16,128]{2,1,0:T(8,128)}), f32[128,16,128]{2,1,0:T(8,128)S(1)}, u32[]{:S(2)}, u32[]{:S(2)}) async-start(f32[128,16,128]{2,1,0:T(8,128)} %bitcast.2), calls=%async_computation | async-start | bytes 2097152 | tf_op jit(solution)/shard_map/all_to_all | solution.py:41
  27.4 224.3 %all-reduce.2.cloned.1.call-start = ((), (), s32[]{:S(2)}) async-start(), calls=%async_computation.2 | async-start | bytes 2097152 | tf_op jit(solution)/shard_map/psum | solution.py:59
  28.2 244.0 %all-gather.2.cloned.1.call-start = ((), (), s32[]{:S(2)}) async-start(), calls=%async_computation.3 | async-start | bytes 3145728 | tf_op jit(solution)/shard_map/all_gather | solution.py:61
  252.9 12.6 %copy-start.6 = (s32[1,3]{1,0:T(1,128)S(1)}, s32[1,3]{1,0:T(1,128)}, u32[]{:S(2)}) copy-start(s32[1,3]{1,0:T(1,128)} %param.14) | copy-start | bytes 40
  252.9 12.7 %copy-start.4 = (bf16[128,4096]{1,0:T(8,128)(2,1)S(1)}, bf16[128,4096]{1,0:T(8,128)(2,1)}, u32[]{:S(2)}) copy-start(bf16[128,4096]{1,0:T(8,128)(2,1)} %param.13) | copy-start | bytes 3145732
  254.5 12.4 %copy-start.5 = (f32[4096]{0:T(1024)S(1)}, f32[4096]{0:T(1024)}, u32[]{:S(2)}) copy-start(f32[4096]{0:T(1024)} %param.15) | copy-start | bytes 49156
  254.5 36.3 %all-to-all-start.1 = ((f32[128,16,128]{2,1,0:T(8,128)}), f32[128,16,128]{2,1,0:T(8,128)}, u32[]{:S(2)}, u32[]{:S(2)}) async-start(f32[128,16,128]{2,1,0:T(8,128)} %copy.54), calls=%async_computation.1 | async-start | bytes 2097152 | tf_op jit(solution)/shard_map/all_to_all | solution.py:49
  275.7 15.2 %copy-start.3 = (bf16[128,2048]{1,0:T(8,128)(2,1)S(1)}, bf16[128,2048]{1,0:T(8,128)(2,1)}, u32[]{:S(2)}) copy-start(bf16[128,2048]{1,0:T(8,128)(2,1)} %param.8) | copy-start | bytes 1572868
  276.4 17.7 %copy-start.2 = (bf16[128,2048]{0,1:T(8,128)(2,1)S(1)}, bf16[128,2048]{0,1:T(8,128)(2,1)}, u32[]{:S(2)}) copy-start(bf16[128,2048]{0,1:T(8,128)(2,1)} %copy-done.1) | copy-start | bytes 1572868
Sparse Core Ops, SparseCore 0:
  34.2 217.5 all-reduce.1
  253.6 18.5 all-gather.1

commit v3 on v2

--- a/solution.py
+++ b/solution.py
@@ -46,8 +46,13 @@
     exclusive = jnp.dot(
         before.astype(jnp.float32), flat, precision=lax.Precision.HIGHEST
     ).reshape(chunks.shape)
-    prefix = lax.all_to_all(exclusive, "seq", 0, 0, tiled=True)
-    return prefix.reshape(local_state.shape)
+    total = jnp.sum(gathered, axis=0, keepdims=True)
+    payload = jnp.concatenate([exclusive, jnp.broadcast_to(total, chunks.shape)], axis=1)
+    back = lax.all_to_all(payload, "seq", 0, 0, tiled=True)
+    half = chunks.shape[1]
+    prefix = back[:, :half].reshape(local_state.shape)
+    total = back[:, half:].reshape(local_state.shape)
+    return prefix, total
 
 
 def per_device(
@@ -56,9 +61,12 @@
     heads_here = cat_query.shape[1] // DH
     all_heads = resp_query.shape[1] // DH
     local_state = block_state(cat_key, cat_value, heads_here)
-    total = lax.psum(local_state, "seq")
-    prefix = transpose_scan(local_state)
-    whole = lax.all_gather(total, "resp", axis=0, tiled=True)
+    prefix, total = transpose_scan(local_state)
+    other = lax.ppermute(total, "resp", [(0, 1), (1, 0)])
+    first = lax.axis_index("resp") == 0
+    whole = jnp.concatenate(
+        [jnp.where(first, total, other), jnp.where(first, other, total)], axis=0
+    )
 
     places = jnp.arange(cat_query.shape[0], dtype=jnp.int32)
     causal = places[None, :] <= places[:, None]

time: 309 us -> 142 us (0.46); the launches traced: 304 us -> 141 us
  waiting for transfers between devices: 239 us -> 45.4 us
  blocking collectives: 0 us -> 46.4 us
  starting transfers between devices: 27.4 us -> 12.1 us
  between operations: 14.2 us -> 0.78 us
  local copies, waits for them, and re-layouts: 7.08 us -> 15.7 us
  other arithmetic: 1.44 us -> 5.47 us
    psum x1 -> x0, waiting for transfers between devices: 224 us -> none  [per_device(): total = lax.psum(local_state, 'seq')]
    all_to_all x0 -> x1, blocking collectives: none -> 46.4 us  [transpose_scan(): gathered = lax.all_to_all(chunks, 'seq', 0, 0, tiled=True)]
    all_to_all x2 -> x1, waiting for transfers between devices: 13.1 us -> 45.4 us  [transpose_scan(): back = lax.all_to_all(payload, 'seq', 0, 0, tiled=True)]
    all_to_all x2 -> x1, starting transfers between devices: 27.3 us -> 7.47 us  [transpose_scan(): back = lax.all_to_all(payload, 'seq', 0, 0, tiled=True)]
    ppermute x0 -> x1, starting transfers between devices: none -> 4.65 us  [per_device(): other = lax.ppermute(total, 'resp', [(0, 1), (1, 0)])]
  transfers between devices with their start and end apart: 4 -> 2, of which waited for: 3 -> 1; matrix products, arithmetic and copies ran while one was open for 4% -> 11% of each run, Pallas kernels for 0% -> 0%
where the time goes in v3:
time: 142 us; the launch traced here: 141 us
  blocking collectives  46.4 us (33%)
  waiting for transfers between devices  45.4 us (32%)
  local copies, waits for them, and re-layouts  15.7 us (11%)
  matrix products  15.3 us (11%)
  starting transfers between devices  12.1 us (9%)
  other arithmetic  5.47 us (4%)
    all_to_all x1, blocking collectives, transpose_scan(): gathered = lax.all_to_all(chunks, 'seq', 0, 0, tiled=True)  46.4 us
    all_to_all x1, waiting for transfers between devices, transpose_scan(): back = lax.all_to_all(payload, 'seq', 0, 0, tiled=True)  45.4 us
    all_to_all x1, starting transfers between devices, transpose_scan(): back = lax.all_to_all(payload, 'seq', 0, 0, tiled=True)  7.47 us
    dot_general x2, matrix products, attend_inner(): jnp.einsum('hts,shd->thd', scores, vh, preferred_element_type=jnp.float32)  6.45 us
    dot_general x2, matrix products, attend_outer(): jnp.einsum('thd,hde->the', qh, state, precision=lax.Precision.HIGHEST)  5.65 us
    ppermute x1, starting transfers between devices, per_device(): other = lax.ppermute(total, 'resp', [(0, 1), (1, 0)])  4.65 us
    unnamed x14, local copies, waits for them, and re-layouts  4.39 us
    convert_element_type x2, other arithmetic, head_norm(): return scaled.reshape(raw.shape[0], heads * DH).astype(jnp.bfloat16)  3.08 us
  transfers between devices with their start and end apart: 2, of which 1 were waited for; matrix products, arithmetic and copies ran while one was open for 11% of the time, Pallas kernels for 0%

profile of v3, /device:TPU:1, one launch (start us, length us, event | category | flops | bytes accessed | tf_op | source)
XLA Modules:
  0.0 141.1 jit_solution(1934947331740640505)
XLA Ops:
  0.6 0.0 copy-start
  0.6 1.4 copy.73
  2.0 0.0 copy-start.1
  2.1 1.5 %fusion.24 = f32[16,128,128]{2,1,0:T(8,128)S(1)} fusion(bf16[128,16,128]{0,2,1:T(8,128)(2,1)S(1)} %bitcast.91, bf16[128,2048]{1,0:T(8,128)(2,1)} %param.10), kind=kOutput, calls=%fused_computation.28 | convolution fusion | flops 67108864 | bytes 2097152 | tf_op jit(solution)/shard_map/shd,she->hde/dot_general | solution.py:29
  3.6 0.0 copy-done.1
  3.6 46.4 %all_to_all.10 = f32[128,16,128]{2,1,0:T(8,128)S(1)} all-to-all(f32[128,16,128]{2,1,0:T(8,128)S(1)} %bitcast.95), channel_id=1, replica_groups=mesh['seq'=128,'resp'=2] {'seq'}, dimensions={0} | all-to-all | bytes 2097152 | tf_op jit(solution)/shard_map/all_to_all | solution.py:41
  50.0 0.4 copy.71
  50.4 1.6 %fusion.16 = f32[128,16,128]{2,0,1:T(8,128)} fusion(f32[128,16,128]{0,2,1:T(8,128)S(1)} %copy.71), kind=kOutput, calls=%fused_computation.19 | convolution fusion | flops 402669568 | bytes 2097152 | tf_op jit(solution)/shard_map/dot_general | solution.py:46
  52.1 0.0 copy-start.2
  52.1 0.1 reduce_sum.36
  52.2 0.1 broadcast_in_dim.24
  52.3 1.0 copy-done.2
  53.3 0.2 pad_maximum_fusion
  53.5 2.5 %copy.58 = f32[128,32,128]{2,1,0:T(8,128)} copy(f32[128,32,128]{2,0,1:T(8,128)S(1)} %pad_maximum_fusion) | data formatting | bytes 4194304 | tf_op jit(solution)/shard_map/concatenate | solution.py:50
  56.0 0.0 copy-start.5
  56.0 0.0 copy-start.3
  56.0 7.5 %all-to-all-start.1 = ((f32[128,32,128]{2,1,0:T(8,128)}), f32[128,32,128]{2,1,0:T(8,128)}, u32[]{:S(2)}, u32[]{:S(2)}) async-start(f32[128,32,128]{2,1,0:T(8,128)} %copy.58), calls=%async_computation.1 | async-start | bytes 4194304 | tf_op jit(solution)/shard_map/all_to_all | solution.py:51
  63.5 0.0 copy-start.4
  63.5 0.0 copy-done.5
  63.5 0.2 reduce-window.8
  63.7 0.0 copy-done.3
  63.7 1.3 copy.72
  65.0 0.0 copy-done.4
  65.0 0.1 convert_reduce_fusion
  65.1 0.1 compare_and_fusion
  65.2 0.0 copy-done
  65.2 3.1 %fusion.6 = f32[32,128,128]{1,2,0:T(8,128)S(1)} fusion(bf16[128,32,128]{0,2,1:T(8,128)(2,1)} %bitcast.93, pred[128,128]{1,0:T(8,128)(4,1)S(1)} %compare_and_fusion, bf16[128,4096]{1,0:T(8,128)(2,1)} %param.12, bf16[128,4096]{1,0:T(8,128)(2,1)S(1)} %copy-done), kind=kOutput, calls=%fused_computation.10 | convolution fusion | flops 269484032 | bytes 5259264 | tf_op jit(solution)/shard_map/hts,shd->thd/dot_general | solution.py:16
  68.3 45.4 %all-to-all-done.1 = f32[128,32,128]{2,1,0:T(8,128)} async-done(((f32[128,32,128]{2,1,0:T(8,128)}), f32[128,32,128]{2,1,0:T(8,128)}, u32[]{:S(2)}, u32[]{:S(2)}) %all-to-all-start.1) | async-done | bytes 2097184 | tf_op jit(solution)/shard_map/all_to_all | solution.py:51
  113.8 3.0 %fusion.41 = (f32[128,16,128]{2,1,0:T(8,128)}, f32[128,16,128]{2,1,0:T(8,128)}) fusion(f32[128,32,128]{2,1,0:T(8,128)} %all-to-all-done.1), kind=kLoop, calls=%fused_computation.52 | loop fusion | bytes 4194304 | tf_op jit(solution)/shard_map/slice | solution.py:54
  116.8 2.5 %copy.65 = f32[16,128,128]{1,2,0:T(8,128)} copy(f32[16,128,128]{2,1,0:T(8,128)} %bitcast.97) | data formatting | bytes 2097152 | tf_op jit(solution)/shard_map/reshape | solution.py:54
  119.3 4.6 %collective-permute-start = (f32[16,128,128]{1,2,0:T(8,128)}, f32[16,128,128]{1,2,0:T(8,128)}, u32[]{:S(2)}, u32[]{:S(2)}) collective-permute-start(f32[16,128,128]{1,2,0:T(8,128)} %copy.65), channel_id=1, source_target_pairs={{0,1},{1,0},{2,3},{3,2},{4,5},{5,4},{6,7},{7,6},{8,9},{9,8},{10,11... | collective-permute-start | bytes 3145736 | tf_op jit(solution)/shard_map/ppermute | solution.py:65
  124.0 3.3 %convolution_bitcast_fusion.1 = f32[128,16,128]{0,2,1:T(8,128)} fusion(f32[16,128,128]{2,1,0:T(8,128)} %bitcast.96, bf16[128,2048]{1,0:T(8,128)(2,1)} %param.8), kind=kOutput, calls=%fused_computation.13 | convolution fusion | flops 402653184 | bytes 2621440 | tf_op jit(solution)/shard_map/thd,hde->the/dot_general | solution.py:22
  127.3 3.3 %multiply_reduce_fusion.1 = (f32[128,16]{0,1:T(8,128)S(1)}, f32[128,16,128]{0,2,1:T(8,128)}) fusion(f32[128,16,128]{0,2,1:T(8,128)} %convolution_bitcast_fusion.1, bf16[128,16,128]{0,2,1:T(8,128)(2,1)} %bitcast.92, pred[128,128]{1,0:T(8,128)(4,1)S(1)} %iota_compare_fusion.1, bf16[128,2048]{1,0:T(8,128)(2,1)} %param.10, bf16[128,2048]{1,0:T(8,128)(2,1)} %param.8), kind=kOutput, calls=%fused_computation.23 | convolution fusion | flops 135526400 | bytes 3694592 | tf_op jit(solution)/shard_map/hts,shd->thd/dot_general | solution.py:16
  130.7 2.4 %multiply_convert_fusion.1 = bf16[128,16,128]{0,2,1:T(8,128)(2,1)} fusion(f32[128,16,128]{0,2,1:T(8,128)} %get-tuple-element.15, f32[16,128]{1,0:T(8,128)S(1)} %dynamic-slice_bitcast_fusion, f32[128,16]{0,1:T(8,128)S(1)} %add_rsqrt_fusion.1), kind=kLoop, calls=%fused_computation.22 | loop fusion | flops 786432 | bytes 1589248 | tf_op jit(solution)/shard_map/convert_element_type | solution.py:35
  133.0 2.0 %copy.68 = bf16[128,2048]{1,0:T(8,128)(2,1)} copy(bf16[128,2048]{0,1:T(8,128)(2,1)} %bitcast.98) | data formatting | bytes 1048576
  135.1 0.0 collective-permute-done
  135.1 1.7 %broadcast_select_fusion.1 = (f32[16,128,128]{1,2,0:T(8,128)S(1)}, f32[16,128,128]{1,2,0:T(8,128)S(1)}) fusion(f32[16,128,128]{1,2,0:T(8,128)} %copy.65, f32[16,128,128]{1,2,0:T(8,128)} %collective-permute-done, pred[]{:T(512)S(6)} %eq.23), kind=kLoop, calls=%fused_computation.34 | loop fusion | flops 524288 | bytes 4194305 | tf_op jit(solution)/shard_map/jit(_where)/select_n | solution.py:68
  136.8 2.3 %multiply_reduce_fusion = (f32[128,32]{0,1:T(8,128)S(1)}, f32[128,32,128]{0,2,1:T(8,128)S(1)}) fusion(f32[16,128,128]{1,2,0:T(8,128)S(1)} %get-tuple-element.11, f32[16,128,128]{1,2,0:T(8,128)S(1)} %get-tuple-element.10, f32[32,128,128]{1,2,0:T(8,128)S(1)} %fusion.6, bf16[128,4096]{1,0:T(8,128)(2,1)S(1)} %copy-done), kind=kOutput, calls=%fused_computation.7 | convolution fusion | flops 807399424 | bytes 7356416 | tf_op jit(solution)/shard_map/thd,hde->the/dot_general | solution.py:22
  139.1 0.7 multiply_convert_fusion
  139.8 1.3 copy.69
  (4 shorter events, 0.0 us)
Async XLA Ops:
  0.6 64.6 %copy-start = (bf16[128,4096]{1,0:T(8,128)(2,1)S(1)}, bf16[128,4096]{1,0:T(8,128)(2,1)}, u32[]{:S(2)}) copy-start(bf16[128,4096]{1,0:T(8,128)(2,1)} %param.11) | copy-start | bytes 3145732
  2.0 1.5 %copy-start.1 = (bf16[128,2048]{0,1:T(8,128)(2,1)}, bf16[128,2048]{0,1:T(8,128)(2,1)S(1)}, u32[]{:S(2)}) copy-start(bf16[128,2048]{0,1:T(8,128)(2,1)S(1)} %copy.73) | copy-start | bytes 1572868
  52.1 1.2 copy-start.2
  56.0 7.5 %copy-start.5 = (s32[1,3]{1,0:T(1,128)S(1)}, s32[1,3]{1,0:T(1,128)}, u32[]{:S(2)}) copy-start(s32[1,3]{1,0:T(1,128)} %param.14) | copy-start | bytes 40
  56.0 7.7 %copy-start.3 = (bf16[128,4096]{1,0:T(8,128)(2,1)S(1)}, bf16[128,4096]{1,0:T(8,128)(2,1)}, u32[]{:S(2)}) copy-start(bf16[128,4096]{1,0:T(8,128)(2,1)} %param.13) | copy-start | bytes 3145732
  56.0 57.7 %all-to-all-start.1 = ((f32[128,32,128]{2,1,0:T(8,128)}), f32[128,32,128]{2,1,0:T(8,128)}, u32[]{:S(2)}, u32[]{:S(2)}) async-start(f32[128,32,128]{2,1,0:T(8,128)} %copy.58), calls=%async_computation.1 | async-start | bytes 4194304 | tf_op jit(solution)/shard_map/all_to_all | solution.py:51
  63.5 1.5 %copy-start.4 = (f32[4096]{0:T(1024)S(1)}, f32[4096]{0:T(1024)}, u32[]{:S(2)}) copy-start(f32[4096]{0:T(1024)} %param.15) | copy-start | bytes 49156
  119.3 15.7 %collective-permute-start = (f32[16,128,128]{1,2,0:T(8,128)}, f32[16,128,128]{1,2,0:T(8,128)}, u32[]{:S(2)}, u32[]{:S(2)}) collective-permute-start(f32[16,128,128]{1,2,0:T(8,128)} %copy.65), channel_id=1, source_target_pairs={{0,1},{1,0},{2,3},{3,2},{4,5},{5,4},{6,7},{7,6},{8,9},{9,8},{10,11... | collective-permute-start | bytes 3145736 | tf_op jit(solution)/shard_map/ppermute | solution.py:65

commit v4 on v3

--- a/solution.py
+++ b/solution.py
@@ -1,6 +1,8 @@
 import jax
 import jax.numpy as jnp
 from jax import lax
+from jax.experimental import pallas as pl
+from jax.experimental.pallas import tpu as pltpu
 from jax.sharding import PartitionSpec as P
 
 DH = 128
@@ -35,21 +37,80 @@
     return scaled.reshape(raw.shape[0], heads * DH).astype(jnp.bfloat16)
 
 
+def scan_kernel(x_ref, out_ref, got, payload, back, sends, recvs):
+    peers, half = x_ref.shape[0], x_ref.shape[1]
+    me = lax.axis_index("seq")
+    mesh_ids = pl.DeviceIdType.MESH
+
+    def exchange(phase, src, dst):
+        def copy_to(peer, at):
+            return pltpu.make_async_remote_copy(
+                src_ref=src.at[peer],
+                dst_ref=dst.at[at],
+                send_sem=sends.at[phase],
+                recv_sem=recvs.at[phase],
+                device_id={"seq": peer},
+                device_id_type=mesh_ids,
+            )
+
+        def start(t, carry):
+            copy_to(lax.rem(me + t, peers), me).start()
+            return carry
+
+        lax.fori_loop(1, peers, start, 0)
+        dst[pl.ds(me, 1)] = src[pl.ds(me, 1)]
+
+        others = pl.ds(0, peers - 1)
+        everyone = pltpu.make_async_remote_copy(
+            src_ref=src.at[others],
+            dst_ref=dst.at[others],
+            send_sem=sends.at[phase],
+            recv_sem=recvs.at[phase],
+            device_id={"seq": lax.rem(me + 1, peers)},
+            device_id_type=mesh_ids,
+        )
+        everyone.wait_send()
+        everyone.wait_recv()
+
+    exchange(0, x_ref, got)
+
+    def running(j, acc):
+        payload[pl.ds(j, 1), pl.ds(0, half), :] = acc[None]
+        return acc + got[j]
+
+    total = lax.fori_loop(0, peers, running, jnp.zeros((half, DH), jnp.float32), unroll=8)
+
+    def fill(j, carry):
+        payload[pl.ds(j, 1), pl.ds(half, half), :] = total[None]
+        return carry
+
+    lax.fori_loop(0, peers, fill, 0, unroll=8)
+    exchange(1, payload, back)
+    out_ref[...] = back[...]
+
+
 def transpose_scan(local_state):
     peers = lax.axis_size("seq")
     chunks = local_state.reshape(peers, -1, DH)
-    gathered = lax.all_to_all(chunks, "seq", 0, 0, tiled=True)
-    before = lax.broadcasted_iota(jnp.int32, (peers, peers), 1) < lax.broadcasted_iota(
-        jnp.int32, (peers, peers), 0
-    )
-    flat = gathered.reshape(peers, -1)
-    exclusive = jnp.dot(
-        before.astype(jnp.float32), flat, precision=lax.Precision.HIGHEST
-    ).reshape(chunks.shape)
-    total = jnp.sum(gathered, axis=0, keepdims=True)
-    payload = jnp.concatenate([exclusive, jnp.broadcast_to(total, chunks.shape)], axis=1)
-    back = lax.all_to_all(payload, "seq", 0, 0, tiled=True)
     half = chunks.shape[1]
+    vmem = pl.BlockSpec(memory_space=pltpu.VMEM)
+    back = pl.pallas_call(
+        scan_kernel,
+        out_shape=jax.ShapeDtypeStruct((peers, 2 * half, DH), jnp.float32),
+        in_specs=[vmem],
+        out_specs=vmem,
+        scratch_shapes=[
+            pltpu.VMEM((peers, half, DH), jnp.float32),
+            pltpu.VMEM((peers, 2 * half, DH), jnp.float32),
+            pltpu.VMEM((peers, 2 * half, DH), jnp.float32),
+            pltpu.SemaphoreType.DMA((2,)),
+            pltpu.SemaphoreType.DMA((2,)),
+        ],
+        compiler_params=pltpu.CompilerParams(has_side_effects=True),
+        cost_estimate=pl.CostEstimate(
+            flops=2 * peers * half * DH, transcendentals=0, bytes_accessed=12 * peers * half * DH
+        ),
+    )(chunks)
     prefix = back[:, :half].reshape(local_state.shape)
     total = back[:, half:].reshape(local_state.shape)
     return prefix, total

time: 142 us -> 122 us (0.86)
  Pallas kernels: 0 us -> 92.7 us
  blocking collectives: 46.4 us -> 0 us
  waiting for transfers between devices: 45.4 us -> 0.01 us
  starting transfers between devices: 12.1 us -> 1.21 us
  matrix products: 15.3 us -> 11.4 us
  local copies, waits for them, and re-layouts: 15.7 us -> 12.6 us
  other arithmetic: 5.47 us -> 3.12 us
    pallas_call x0 -> x1, Pallas kernels: none -> 92.7 us  [transpose_scan(): pl.pallas_call(scan_kernel, out_shape=jax.ShapeDtypeStruct((peers, 2 * ha...]
    all_to_all x1 -> x0, blocking collectives: 46.4 us -> none  [transpose_scan(): gathered = lax.all_to_all(chunks, 'seq', 0, 0, tiled=True)]
    all_to_all x1 -> x0, waiting for transfers between devices: 45.4 us -> none  [transpose_scan(): back = lax.all_to_all(payload, 'seq', 0, 0, tiled=True)]
    all_to_all x1 -> x0, starting transfers between devices: 7.47 us -> none  [transpose_scan(): back = lax.all_to_all(payload, 'seq', 0, 0, tiled=True)]
    ppermute x1, starting transfers between devices: 4.65 us -> 1.21 us  [per_device(): other = lax.ppermute(total, 'resp', [(0, 1), (1, 0)])]
    concatenate x1 -> x0, local copies, waits for them, and re-layouts: 2.52 us -> none  [transpose_scan(): jnp.concatenate([exclusive, jnp.broadcast_to(total, chunks.shape)], axis=1)]
    reshape x1 -> x2, local copies, waits for them, and re-layouts: 1.4 us -> 3.67 us  [attend_inner(): kh = key.reshape(rows, heads, DH)]
    unnamed x14 -> x12, local copies, waits for them, and re-layouts: 4.39 us -> 2.35 us
  transfers between devices with their start and end apart: 2 -> 1, of which waited for: 1 -> 0; matrix products, arithmetic and copies ran while one was open for 11% -> 10% of each run, Pallas kernels for 0% -> 0%
where the time goes in v4:
time: 122 us
  Pallas kernels  92.7 us (76%)
  local copies, waits for them, and re-layouts  12.6 us (10%)
  matrix products  11.4 us (9%)
  other arithmetic  3.12 us (3%)
    pallas_call x1, Pallas kernels, transpose_scan(): pl.pallas_call(scan_kernel, out_shape=jax.ShapeDtypeStruct((peers, 2 * ha...  92.7 us
    dot_general x2, matrix products, attend_inner(): jnp.einsum('hts,shd->thd', scores, vh, preferred_element_type=jnp.float32)  4.76 us
    dot_general x2, matrix products, attend_outer(): jnp.einsum('thd,hde->the', qh, state, precision=lax.Precision.HIGHEST)  4.29 us
    reshape x2, local copies, waits for them, and re-layouts, attend_inner(): kh = key.reshape(rows, heads, DH)  3.67 us
    slice x1, local copies, waits for them, and re-layouts, transpose_scan(): total = back[:, half:].reshape(local_state.shape)  2.68 us
    reshape x1, local copies, waits for them, and re-layouts, transpose_scan(): total = back[:, half:].reshape(local_state.shape)  2.61 us
  transfers between devices with their start and end apart: 1, of which 0 were waited for; matrix products, arithmetic and copies ran while one was open for 10% of the time, Pallas kernels for 0%

profile of v4, /device:TPU:1, one launch (start us, length us, event | category | flops | bytes accessed | tf_op | source)
XLA Modules:
  0.0 121.8 jit_solution(8972230573385522727)
XLA Ops:
  0.6 0.0 copy-start
  0.6 1.4 %copy.36 = bf16[128,2048]{0,1:T(8,128)(2,1)S(1)} copy(bf16[128,2048]{1,0:T(8,128)(2,1)} %param.9) | data formatting | bytes 1048576 | tf_op jit(solution)/shard_map/reshape | solution.py:14
  2.0 2.3 %fusion.18 = f32[16,128,128]{2,1,0:T(8,128)} fusion(bf16[128,16,128]{0,2,1:T(8,128)(2,1)S(1)} %bitcast.74, bf16[128,2048]{1,0:T(8,128)(2,1)} %param.10), kind=kOutput, calls=%fused_computation.23 | convolution fusion | flops 67108864 | bytes 2097152 | tf_op jit(solution)/shard_map/shd,she->hde/dot_general | solution.py:31
  4.4 92.7 %shard_map.95 = f32[128,32,128]{2,1,0:T(8,128)} custom-call(f32[128,16,128]{2,1,0:T(8,128)} %bitcast.79), custom_call_target="tpu_custom_call" | custom-call | flops 524288 | bytes 3145728 | tf_op jit(solution)/shard_map/pallas_call | solution.py:97
  97.1 2.7 %fusion.33 = (f32[128,16,128]{2,1,0:T(8,128)}, f32[128,16,128]{2,1,0:T(8,128)S(1)}) fusion(f32[128,32,128]{2,1,0:T(8,128)} %shard_map.95), kind=kLoop, calls=%fused_computation.45 | loop fusion | bytes 4194304 | tf_op jit(solution)/shard_map/slice | solution.py:115
  99.8 0.0 copy-start.4
  99.8 0.0 copy-start.1
  99.8 2.6 %copy.29 = f32[16,128,128]{1,2,0:T(8,128)} copy(f32[16,128,128]{2,1,0:T(8,128)} %bitcast.81) | data formatting | bytes 2097152 | tf_op jit(solution)/shard_map/reshape | solution.py:115
  102.4 1.2 collective-permute-start
  103.6 0.0 copy-done.4
  103.6 0.2 reduce-window.8
  103.8 0.0 copy-done.1
  103.8 2.0 %convolution_bitcast_fusion.1 = f32[128,16,128]{0,2,1:T(8,128)} fusion(f32[16,128,128]{2,1,0:T(8,128)S(1)} %bitcast.80, bf16[128,2048]{1,0:T(8,128)(2,1)S(1)} %copy-done.1), kind=kOutput, calls=%fused_computation.12 | convolution fusion | flops 402653184 | bytes 2621440 | tf_op jit(solution)/shard_map/thd,hde->the/dot_general | solution.py:24
  105.8 0.0 copy-start.3
  105.8 2.1 %multiply_reduce_fusion.1 = (f32[128,16]{0,1:T(8,128)S(1)}, f32[128,16,128]{0,2,1:T(8,128)S(1)}) fusion(f32[128,16,128]{0,2,1:T(8,128)} %convolution_bitcast_fusion.1, bf16[128,16,128]{0,2,1:T(8,128)(2,1)S(1)} %bitcast.75, pred[128,128]{1,0:T(8,128)(4,1)S(1)} %iota_compare_fusion, bf16[128,2048]{1,0:T(8,128)(2,1)} %param.10, bf16[128,2048]{1,0:T(8,128)(2,1)S(1)} %copy-done.1), kind=kOutput, calls=%fused_computation.18 | convolution fusion | flops 135526400 | bytes 3694592 | tf_op jit(solution)/shard_map/hts,shd->thd/dot_general | solution.py:18
  107.8 0.0 copy-done.3
  107.9 0.3 multiply_convert_fusion.1
  108.2 0.0 copy-start.2
  108.2 1.0 copy.32
  109.2 2.3 %copy.37 = bf16[128,4096]{0,1:T(8,128)(2,1)} copy(bf16[128,4096]{1,0:T(8,128)(2,1)} %param.12) | data formatting | bytes 2097152 | tf_op jit(solution)/shard_map/reshape | solution.py:14
  111.5 0.0 copy-done.2
  111.5 1.3 %copy.38 = bf16[128,4096]{0,1:T(8,128)(2,1)} copy(bf16[128,4096]{1,0:T(8,128)(2,1)S(1)} %copy-done.2) | data formatting | bytes 2097152 | tf_op jit(solution)/shard_map/reshape | solution.py:15
  112.8 0.1 convert_reduce_fusion
  112.9 0.1 compare_and_fusion
  113.0 0.0 copy-done
  113.0 2.7 %fusion.6 = f32[32,128,128]{1,2,0:T(8,128)S(1)} fusion(bf16[128,32,128]{0,2,1:T(8,128)(2,1)} %bitcast.77, bf16[128,32,128]{0,2,1:T(8,128)(2,1)} %bitcast.76, pred[128,128]{1,0:T(8,128)(4,1)S(1)} %compare_and_fusion, bf16[128,4096]{1,0:T(8,128)(2,1)S(1)} %copy-done), kind=kOutput, calls=%fused_computation.9 | convolution fusion | flops 269484032 | bytes 5259264 | tf_op jit(solution)/shard_map/hts,shd->thd/dot_general | solution.py:18
  115.7 0.0 collective-permute-done
  115.7 1.7 %broadcast_select_fusion.1 = (f32[16,128,128]{1,2,0:T(8,128)S(1)}, f32[16,128,128]{1,2,0:T(8,128)S(1)}) fusion(f32[16,128,128]{1,2,0:T(8,128)} %copy.29, f32[16,128,128]{1,2,0:T(8,128)} %collective-permute-done, pred[]{:T(512)S(6)} %eq.23), kind=kLoop, calls=%fused_computation.29 | loop fusion | flops 524288 | bytes 4194305 | tf_op jit(solution)/shard_map/jit(_where)/select_n | solution.py:129
  117.4 2.3 %multiply_reduce_fusion = (f32[128,32]{0,1:T(8,128)S(1)}, f32[128,32,128]{0,2,1:T(8,128)S(1)}) fusion(f32[16,128,128]{1,2,0:T(8,128)S(1)} %get-tuple-element.7, f32[16,128,128]{1,2,0:T(8,128)S(1)} %get-tuple-element.6, f32[32,128,128]{1,2,0:T(8,128)S(1)} %fusion.6, bf16[128,4096]{1,0:T(8,128)(2,1)S(1)} %copy-done), kind=kOutput, calls=%fused_computation.6 | convolution fusion | flops 807399424 | bytes 7356416 | tf_op jit(solution)/shard_map/thd,hde->the/dot_general | solution.py:24
  119.7 0.7 multiply_convert_fusion
  120.5 1.3 %copy.33 = bf16[128,4096]{1,0:T(8,128)(2,1)} copy(bf16[128,4096]{0,1:T(8,128)(2,1)S(1)} %bitcast.78) | data formatting | bytes 2097152
  (4 shorter events, 0.0 us)
Async XLA Ops:
  0.6 112.4 %copy-start = (bf16[128,4096]{1,0:T(8,128)(2,1)S(1)}, bf16[128,4096]{1,0:T(8,128)(2,1)}, u32[]{:S(2)}) copy-start(bf16[128,4096]{1,0:T(8,128)(2,1)} %param.11) | copy-start | bytes 3145732
  99.8 3.8 %copy-start.4 = (s32[1,3]{1,0:T(1,128)S(1)}, s32[1,3]{1,0:T(1,128)}, u32[]{:S(2)}) copy-start(s32[1,3]{1,0:T(1,128)} %param.14) | copy-start | bytes 40
  99.8 4.0 %copy-start.1 = (bf16[128,2048]{1,0:T(8,128)(2,1)S(1)}, bf16[128,2048]{1,0:T(8,128)(2,1)}, u32[]{:S(2)}) copy-start(bf16[128,2048]{1,0:T(8,128)(2,1)} %param.8) | copy-start | bytes 1572868
  102.4 13.3 %collective-permute-start = (f32[16,128,128]{1,2,0:T(8,128)}, f32[16,128,128]{1,2,0:T(8,128)}, u32[]{:S(2)}, u32[]{:S(2)}) collective-permute-start(f32[16,128,128]{1,2,0:T(8,128)} %copy.29), channel_id=1, source_target_pairs={{0,1},{1,0},{2,3},{3,2},{4,5},{5,4},{6,7},{7,6},{8,9},{9,8},{10,11... | collective-permute-start | bytes 3145736 | tf_op jit(solution)/shard_map/ppermute | solution.py:126
  105.8 2.1 %copy-start.3 = (f32[4096]{0:T(1024)S(1)}, f32[4096]{0:T(1024)}, u32[]{:S(2)}) copy-start(f32[4096]{0:T(1024)} %param.15) | copy-start | bytes 49156
  108.2 3.3 %copy-start.2 = (bf16[128,4096]{1,0:T(8,128)(2,1)S(1)}, bf16[128,4096]{1,0:T(8,128)(2,1)}, u32[]{:S(2)}) copy-start(bf16[128,4096]{1,0:T(8,128)(2,1)} %param.13) | copy-start | bytes 3145732

commit v5 on v4

--- a/solution.py
+++ b/solution.py
@@ -53,7 +53,8 @@
                 device_id_type=mesh_ids,
             )
 
-        def start(t, carry):
+        def start(i, carry):
+            t = jnp.where(i % 2 == 1, (i + 1) // 2, peers - i // 2)
             copy_to(lax.rem(me + t, peers), me).start()
             return carry
 

time: 122 us -> 126 us (1.033)
  Pallas kernels: 92.7 us -> 95.4 us
    pallas_call x1, Pallas kernels: 92.7 us -> 95.4 us  [transpose_scan(): pl.pallas_call(scan_kernel, out_shape=jax.ShapeDtypeStruct((peers, 2 * ha...]
where the time goes in v5:
time: 126 us; the launch traced here: 125 us
  Pallas kernels  95.4 us (76%)
  local copies, waits for them, and re-layouts  12.6 us (10%)
  matrix products  11.4 us (9%)
  other arithmetic  3.12 us (2%)
  starting transfers between devices  1.97 us (2%)
    pallas_call x1, Pallas kernels, transpose_scan(): pl.pallas_call(scan_kernel, out_shape=jax.ShapeDtypeStruct((peers, 2 * ha...  95.4 us
    dot_general x2, matrix products, attend_inner(): jnp.einsum('hts,shd->thd', scores, vh, preferred_element_type=jnp.float32)  4.76 us
    dot_general x2, matrix products, attend_outer(): jnp.einsum('thd,hde->the', qh, state, precision=lax.Precision.HIGHEST)  4.29 us
    reshape x2, local copies, waits for them, and re-layouts, attend_inner(): kh = key.reshape(rows, heads, DH)  3.67 us
    slice x1, local copies, waits for them, and re-layouts, transpose_scan(): total = back[:, half:].reshape(local_state.shape)  2.68 us
    reshape x1, local copies, waits for them, and re-layouts, transpose_scan(): total = back[:, half:].reshape(local_state.shape)  2.61 us
  transfers between devices with their start and end apart: 1, of which 0 were waited for; matrix products, arithmetic and copies ran while one was open for 10% of the time, Pallas kernels for 0%

profile of v5, /device:TPU:1, one launch (start us, length us, event | category | flops | bytes accessed | tf_op | source)
XLA Modules:
  0.0 125.2 jit_solution(14911499511673300024)
XLA Ops:
  0.6 0.0 copy-start
  0.6 1.4 %copy.36 = bf16[128,2048]{0,1:T(8,128)(2,1)S(1)} copy(bf16[128,2048]{1,0:T(8,128)(2,1)} %param.9) | data formatting | bytes 1048576 | tf_op jit(solution)/shard_map/reshape | solution.py:14
  2.0 2.3 %fusion.18 = f32[16,128,128]{2,1,0:T(8,128)} fusion(bf16[128,16,128]{0,2,1:T(8,128)(2,1)S(1)} %bitcast.74, bf16[128,2048]{1,0:T(8,128)(2,1)} %param.10), kind=kOutput, calls=%fused_computation.23 | convolution fusion | flops 67108864 | bytes 2097152 | tf_op jit(solution)/shard_map/shd,she->hde/dot_general | solution.py:31
  4.4 95.4 %shard_map.95 = f32[128,32,128]{2,1,0:T(8,128)} custom-call(f32[128,16,128]{2,1,0:T(8,128)} %bitcast.79), custom_call_target="tpu_custom_call" | custom-call | flops 524288 | bytes 3145728 | tf_op jit(solution)/shard_map/pallas_call | solution.py:98
  99.8 2.7 %fusion.33 = (f32[128,16,128]{2,1,0:T(8,128)}, f32[128,16,128]{2,1,0:T(8,128)S(1)}) fusion(f32[128,32,128]{2,1,0:T(8,128)} %shard_map.95), kind=kLoop, calls=%fused_computation.45 | loop fusion | bytes 4194304 | tf_op jit(solution)/shard_map/slice | solution.py:116
  102.5 0.0 copy-start.4
  102.5 0.0 copy-start.1
  102.5 2.6 %copy.29 = f32[16,128,128]{1,2,0:T(8,128)} copy(f32[16,128,128]{2,1,0:T(8,128)} %bitcast.81) | data formatting | bytes 2097152 | tf_op jit(solution)/shard_map/reshape | solution.py:116
  105.1 2.0 %collective-permute-start = (f32[16,128,128]{1,2,0:T(8,128)}, f32[16,128,128]{1,2,0:T(8,128)}, u32[]{:S(2)}, u32[]{:S(2)}) collective-permute-start(f32[16,128,128]{1,2,0:T(8,128)} %copy.29), channel_id=1, source_target_pairs={{0,1},{1,0},{2,3},{3,2},{4,5},{5,4},{6,7},{7,6},{8,9},{9,8},{10,11... | collective-permute-start | bytes 3145736 | tf_op jit(solution)/shard_map/ppermute | solution.py:127
  107.1 0.0 copy-done.4
  107.1 0.2 reduce-window.8
  107.3 0.0 copy-done.1
  107.3 2.0 %convolution_bitcast_fusion.1 = f32[128,16,128]{0,2,1:T(8,128)} fusion(f32[16,128,128]{2,1,0:T(8,128)S(1)} %bitcast.80, bf16[128,2048]{1,0:T(8,128)(2,1)S(1)} %copy-done.1), kind=kOutput, calls=%fused_computation.12 | convolution fusion | flops 402653184 | bytes 2621440 | tf_op jit(solution)/shard_map/thd,hde->the/dot_general | solution.py:24
  109.2 0.0 copy-start.3
  109.2 2.1 %multiply_reduce_fusion.1 = (f32[128,16]{0,1:T(8,128)S(1)}, f32[128,16,128]{0,2,1:T(8,128)S(1)}) fusion(f32[128,16,128]{0,2,1:T(8,128)} %convolution_bitcast_fusion.1, bf16[128,16,128]{0,2,1:T(8,128)(2,1)S(1)} %bitcast.75, pred[128,128]{1,0:T(8,128)(4,1)S(1)} %iota_compare_fusion, bf16[128,2048]{1,0:T(8,128)(2,1)} %param.10, bf16[128,2048]{1,0:T(8,128)(2,1)S(1)} %copy-done.1), kind=kOutput, calls=%fused_computation.18 | convolution fusion | flops 135526400 | bytes 3694592 | tf_op jit(solution)/shard_map/hts,shd->thd/dot_general | solution.py:18
  111.3 0.0 copy-done.3
  111.3 0.3 multiply_convert_fusion.1
  111.7 0.0 copy-start.2
  111.7 1.0 copy.32
  112.7 2.3 %copy.37 = bf16[128,4096]{0,1:T(8,128)(2,1)} copy(bf16[128,4096]{1,0:T(8,128)(2,1)} %param.12) | data formatting | bytes 2097152 | tf_op jit(solution)/shard_map/reshape | solution.py:14
  115.0 0.0 copy-done.2
  115.0 1.3 %copy.38 = bf16[128,4096]{0,1:T(8,128)(2,1)} copy(bf16[128,4096]{1,0:T(8,128)(2,1)S(1)} %copy-done.2) | data formatting | bytes 2097152 | tf_op jit(solution)/shard_map/reshape | solution.py:15
  116.3 0.1 convert_reduce_fusion
  116.4 0.1 compare_and_fusion
  116.5 0.0 copy-done
  116.5 2.7 %fusion.6 = f32[32,128,128]{1,2,0:T(8,128)S(1)} fusion(bf16[128,32,128]{0,2,1:T(8,128)(2,1)} %bitcast.77, bf16[128,32,128]{0,2,1:T(8,128)(2,1)} %bitcast.76, pred[128,128]{1,0:T(8,128)(4,1)S(1)} %compare_and_fusion, bf16[128,4096]{1,0:T(8,128)(2,1)S(1)} %copy-done), kind=kOutput, calls=%fused_computation.9 | convolution fusion | flops 269484032 | bytes 5259264 | tf_op jit(solution)/shard_map/hts,shd->thd/dot_general | solution.py:18
  119.2 0.0 collective-permute-done
  119.2 1.7 %broadcast_select_fusion.1 = (f32[16,128,128]{1,2,0:T(8,128)S(1)}, f32[16,128,128]{1,2,0:T(8,128)S(1)}) fusion(f32[16,128,128]{1,2,0:T(8,128)} %copy.29, f32[16,128,128]{1,2,0:T(8,128)} %collective-permute-done, pred[]{:T(512)S(6)} %eq.23), kind=kLoop, calls=%fused_computation.29 | loop fusion | flops 524288 | bytes 4194305 | tf_op jit(solution)/shard_map/jit(_where)/select_n | solution.py:130
  120.9 2.3 %multiply_reduce_fusion = (f32[128,32]{0,1:T(8,128)S(1)}, f32[128,32,128]{0,2,1:T(8,128)S(1)}) fusion(f32[16,128,128]{1,2,0:T(8,128)S(1)} %get-tuple-element.7, f32[16,128,128]{1,2,0:T(8,128)S(1)} %get-tuple-element.6, f32[32,128,128]{1,2,0:T(8,128)S(1)} %fusion.6, bf16[128,4096]{1,0:T(8,128)(2,1)S(1)} %copy-done), kind=kOutput, calls=%fused_computation.6 | convolution fusion | flops 807399424 | bytes 7356416 | tf_op jit(solution)/shard_map/thd,hde->the/dot_general | solution.py:24
  123.2 0.7 multiply_convert_fusion
  123.9 1.3 %copy.33 = bf16[128,4096]{1,0:T(8,128)(2,1)} copy(bf16[128,4096]{0,1:T(8,128)(2,1)S(1)} %bitcast.78) | data formatting | bytes 2097152
  (4 shorter events, 0.0 us)
Async XLA Ops:
  0.6 115.8 %copy-start = (bf16[128,4096]{1,0:T(8,128)(2,1)S(1)}, bf16[128,4096]{1,0:T(8,128)(2,1)}, u32[]{:S(2)}) copy-start(bf16[128,4096]{1,0:T(8,128)(2,1)} %param.11) | copy-start | bytes 3145732
  102.5 4.6 %copy-start.4 = (s32[1,3]{1,0:T(1,128)S(1)}, s32[1,3]{1,0:T(1,128)}, u32[]{:S(2)}) copy-start(s32[1,3]{1,0:T(1,128)} %param.14) | copy-start | bytes 40
  102.5 4.8 %copy-start.1 = (bf16[128,2048]{1,0:T(8,128)(2,1)S(1)}, bf16[128,2048]{1,0:T(8,128)(2,1)}, u32[]{:S(2)}) copy-start(bf16[128,2048]{1,0:T(8,128)(2,1)} %param.8) | copy-start | bytes 1572868
  105.1 14.1 %collective-permute-start = (f32[16,128,128]{1,2,0:T(8,128)}, f32[16,128,128]{1,2,0:T(8,128)}, u32[]{:S(2)}, u32[]{:S(2)}) collective-permute-start(f32[16,128,128]{1,2,0:T(8,128)} %copy.29), channel_id=1, source_target_pairs={{0,1},{1,0},{2,3},{3,2},{4,5},{5,4},{6,7},{7,6},{8,9},{9,8},{10,11... | collective-permute-start | bytes 3145736 | tf_op jit(solution)/shard_map/ppermute | solution.py:127
  109.2 2.1 %copy-start.3 = (f32[4096]{0:T(1024)S(1)}, f32[4096]{0:T(1024)}, u32[]{:S(2)}) copy-start(f32[4096]{0:T(1024)} %param.15) | copy-start | bytes 49156
  111.7 3.3 %copy-start.2 = (bf16[128,4096]{1,0:T(8,128)(2,1)S(1)}, bf16[128,4096]{1,0:T(8,128)(2,1)}, u32[]{:S(2)}) copy-start(bf16[128,4096]{1,0:T(8,128)(2,1)} %param.13) | copy-start | bytes 3145732

commit v6 on v4

--- a/solution.py
+++ b/solution.py
@@ -37,7 +37,23 @@
     return scaled.reshape(raw.shape[0], heads * DH).astype(jnp.bfloat16)
 
 
-def scan_kernel(x_ref, out_ref, got, payload, back, sends, recvs):
+def heads_inner(q_ref, k_ref, v_ref, keep, o_ref):
+    def one(h, carry):
+        cols = pl.ds(pl.multiple_of(h * DH, DH), DH)
+        scores = lax.dot_general(
+            q_ref[:, cols], k_ref[:, cols], (((1,), (1,)), ((), ())),
+            preferred_element_type=jnp.float32,
+        )
+        scores = jnp.where(keep, scores, 0.0).astype(jnp.bfloat16)
+        o_ref[:, cols] = jnp.dot(scores, v_ref[:, cols], preferred_element_type=jnp.float32)
+        return carry
+
+    lax.fori_loop(0, q_ref.shape[1] // DH, one, 0)
+
+
+def scan_kernel(
+    x_ref, cq, ck, cv, rq, rk, rv, rmask, out_ref, cat_ref, resp_ref, got, payload, back, sends, recvs
+):
     peers, half = x_ref.shape[0], x_ref.shape[1]
     me = lax.axis_index("seq")
     mesh_ids = pl.DeviceIdType.MESH
@@ -59,6 +75,12 @@
 
         lax.fori_loop(1, peers, start, 0)
         dst[pl.ds(me, 1)] = src[pl.ds(me, 1)]
+        if phase == 0:
+            rows = lax.broadcasted_iota(jnp.int32, (cq.shape[0], cq.shape[0]), 0)
+            cols = lax.broadcasted_iota(jnp.int32, (cq.shape[0], cq.shape[0]), 1)
+            heads_inner(cq, ck, cv, cols <= rows, cat_ref)
+        else:
+            heads_inner(rq, rk, rv, rmask[...] != 0, resp_ref)
 
         others = pl.ds(0, peers - 1)
         everyone = pltpu.make_async_remote_copy(
@@ -89,16 +111,20 @@
     out_ref[...] = back[...]
 
 
-def transpose_scan(local_state):
+def transpose_scan(local_state, cat, resp, rmask):
     peers = lax.axis_size("seq")
     chunks = local_state.reshape(peers, -1, DH)
     half = chunks.shape[1]
     vmem = pl.BlockSpec(memory_space=pltpu.VMEM)
-    back = pl.pallas_call(
+    back, cat_inner, resp_inner = pl.pallas_call(
         scan_kernel,
-        out_shape=jax.ShapeDtypeStruct((peers, 2 * half, DH), jnp.float32),
-        in_specs=[vmem],
-        out_specs=vmem,
+        out_shape=(
+            jax.ShapeDtypeStruct((peers, 2 * half, DH), jnp.float32),
+            jax.ShapeDtypeStruct(cat[0].shape, jnp.float32),
+            jax.ShapeDtypeStruct(resp[0].shape, jnp.float32),
+        ),
+        in_specs=[vmem] * 8,
+        out_specs=(vmem, vmem, vmem),
         scratch_shapes=[
             pltpu.VMEM((peers, half, DH), jnp.float32),
             pltpu.VMEM((peers, 2 * half, DH), jnp.float32),
@@ -108,12 +134,14 @@
         ],
         compiler_params=pltpu.CompilerParams(has_side_effects=True),
         cost_estimate=pl.CostEstimate(
-            flops=2 * peers * half * DH, transcendentals=0, bytes_accessed=12 * peers * half * DH
+            flops=4 * DH * (cat[0].shape[0] * cat[0].shape[1] + resp[0].shape[0] * resp[0].shape[1]),
+            transcendentals=0,
+            bytes_accessed=12 * peers * half * DH,
         ),
-    )(chunks)
+    )(chunks, *cat, *resp, rmask)
     prefix = back[:, :half].reshape(local_state.shape)
     total = back[:, half:].reshape(local_state.shape)
-    return prefix, total
+    return prefix, total, cat_inner, resp_inner
 
 
 def per_device(
@@ -122,27 +150,27 @@
     heads_here = cat_query.shape[1] // DH
     all_heads = resp_query.shape[1] // DH
     local_state = block_state(cat_key, cat_value, heads_here)
-    prefix, total = transpose_scan(local_state)
+    rows = jnp.arange(resp_query.shape[0], dtype=jnp.int32)
+    ends = jnp.cumsum(resp_lengths[0])
+    segment = jnp.sum((rows[:, None] >= ends[None, :]).astype(jnp.int32), axis=1)
+    mask = (segment[:, None] == segment[None, :]) & (rows[None, :] <= rows[:, None])
+    prefix, total, cat_inner, resp_inner = transpose_scan(
+        local_state,
+        (cat_query, cat_key, cat_value),
+        (resp_query, resp_key, resp_value),
+        mask.astype(jnp.int32),
+    )
     other = lax.ppermute(total, "resp", [(0, 1), (1, 0)])
     first = lax.axis_index("resp") == 0
     whole = jnp.concatenate(
         [jnp.where(first, total, other), jnp.where(first, other, total)], axis=0
     )
 
-    places = jnp.arange(cat_query.shape[0], dtype=jnp.int32)
-    causal = places[None, :] <= places[:, None]
-    cat_inner = attend_inner(cat_query, cat_key, cat_value, causal, heads_here)
-    rows = jnp.arange(resp_query.shape[0], dtype=jnp.int32)
-    ends = jnp.cumsum(resp_lengths[0])
-    segment = jnp.sum((rows[:, None] >= ends[None, :]).astype(jnp.int32), axis=1)
-    mask = (segment[:, None] == segment[None, :]) & (rows[None, :] <= rows[:, None])
-    resp_inner = attend_inner(resp_query, resp_key, resp_value, mask, all_heads)
-
-    cat_raw = cat_inner + attend_outer(cat_query, prefix, heads_here)
+    cat_raw = cat_inner.reshape(-1, heads_here, DH) + attend_outer(cat_query, prefix, heads_here)
     offset = lax.axis_index("resp") * (heads_here * DH)
     cat_gain = lax.dynamic_slice_in_dim(norm_gain, offset, heads_here * DH)
     cat_out = head_norm(cat_raw, cat_gain, heads_here)
-    resp_raw = resp_inner + attend_outer(resp_query, whole, all_heads)
+    resp_raw = resp_inner.reshape(-1, all_heads, DH) + attend_outer(resp_query, whole, all_heads)
     resp_out = head_norm(resp_raw, norm_gain, all_heads)
     return (cat_out, resp_out)
 

time: 122 us -> 117 us (0.959)
  matrix products: 11.4 us -> 6.7 us
  local copies, waits for them, and re-layouts: 12.6 us -> 9.16 us
  Pallas kernels: 92.7 us -> 94.9 us
    dot_general x2 -> x0, matrix products: 4.76 us -> none  [attend_inner(): jnp.einsum('hts,shd->thd', scores, vh, preferred_element_type=jnp.float32)]
    reshape x1, local copies, waits for them, and re-layouts: 2.61 us -> 0.33 us  [transpose_scan(): total = back[:, half:].reshape(local_state.shape)]
    pallas_call x1, Pallas kernels: 92.7 us -> 94.9 us  [transpose_scan(): pl.pallas_call(scan_kernel, out_shape=(jax.ShapeDtypeStruct((peers, 2 * h...]
  transfers between devices with their start and end apart: 1 -> 1, of which waited for: 0 -> 0; matrix products, arithmetic and copies ran while one was open for 10% -> 6% of each run, Pallas kernels for 0% -> 0%
where the time goes in v6:
time: 117 us
  Pallas kernels  94.9 us (81%)
  local copies, waits for them, and re-layouts  9.16 us (8%)
  matrix products  6.7 us (6%)
  other arithmetic  4.19 us (4%)
  starting transfers between devices  1.29 us (1%)
    pallas_call x1, Pallas kernels, transpose_scan(): pl.pallas_call(scan_kernel, out_shape=(jax.ShapeDtypeStruct((peers, 2 * h...  94.9 us
    dot_general x2, matrix products, attend_outer(): jnp.einsum('thd,hde->the', qh, state, precision=lax.Precision.HIGHEST)  4.39 us
    unnamed x6, local copies, waits for them, and re-layouts  2.35 us
  transfers between devices with their start and end apart: 1, of which 0 were waited for; matrix products, arithmetic and copies ran while one was open for 6% of the time, Pallas kernels for 0%

profile of v6, /device:TPU:1, one launch (start us, length us, event | category | flops | bytes accessed | tf_op | source)
XLA Modules:
  0.0 117.0 jit_solution(3177750451324331778)
XLA Ops:
  0.6 1.3 %copy.35 = bf16[128,2048]{0,1:T(8,128)(2,1)S(1)} copy(bf16[128,2048]{1,0:T(8,128)(2,1)} %ck.1) | data formatting | bytes 1048576 | tf_op jit(solution)/shard_map/reshape | solution.py:29
  1.9 0.8 reduce-window.8
  2.8 0.1 convert_reduce_fusion
  2.9 0.7 fusion.15.rmask
  3.6 2.3 %fusion.11 = f32[16,128,128]{2,1,0:T(8,128)} fusion(bf16[128,16,128]{0,2,1:T(8,128)(2,1)S(1)} %bitcast.53, bf16[128,2048]{1,0:T(8,128)(2,1)} %cv.1), kind=kOutput, calls=%fused_computation.15 | convolution fusion | flops 67108864 | bytes 2097152 | tf_op jit(solution)/shard_map/shd,she->hde/dot_general | solution.py:31
  5.9 94.9 %shard_map.95 = (f32[128,32,128]{2,1,0:T(8,128)}, f32[128,2048]{1,0:T(8,128)}, f32[128,4096]{1,0:T(8,128)}) custom-call(f32[128,16,128]{2,1,0:T(8,128)} %bitcast.50, bf16[128,2048]{1,0:T(8,128)(2,1)} %cq.1, bf16[128,2048]{1,0:T(8,128)(2,1)} %ck.1, bf16[128,2048]{1,0:T(8,128)(2,1)} %cv.1, bf16[128,4096]{1,0:T(8,128)(2,1)} %rq.1, bf16[128,4096]{1,0:T(8,128)(2,1)} %rk.1, ...), custom_call_target="tpu_custom_call" | custom-call | flops 402653184 | bytes 3145728 | tf_op jit(solution)/shard_map/pallas_call | solution.py:119
  100.8 1.7 %fusion.17 = (f32[128,16,128]{2,1,0:T(8,128)S(1)}, f32[128,16,128]{2,1,0:T(8,128)S(1)}) fusion(f32[128,32,128]{2,1,0:T(8,128)} %get-tuple-element.6), kind=kLoop, calls=%fused_computation.29 | loop fusion | bytes 4194304 | tf_op jit(solution)/shard_map/slice | solution.py:143
  102.5 0.0 copy-start.1
  102.5 0.3 copy.28
  102.9 1.3 %collective-permute-start = (f32[16,128,128]{1,2,0:T(8,128)S(1)}, f32[16,128,128]{1,2,0:T(8,128)}, u32[]{:S(2)}, u32[]{:S(2)}) collective-permute-start(f32[16,128,128]{1,2,0:T(8,128)S(1)} %copy.28), channel_id=1, source_target_pairs={{0,1},{1,0},{2,3},{3,2},{4,5},{5,4},{6,7},{7,6},{8,9},{9,8},{10,11... | collective-permute-start | bytes 3145736 | tf_op jit(solution)/shard_map/ppermute | solution.py:163
  104.1 1.5 %copy.36 = f32[128,2048]{0,1:T(8,128)S(1)} copy(f32[128,2048]{1,0:T(8,128)} %get-tuple-element.5) | data formatting | bytes 2097152 | tf_op jit(solution)/shard_map/reshape | solution.py:169
  105.7 0.0 copy-done.1
  105.7 2.1 %multiply_reduce_fusion.1 = (f32[128,16]{0,1:T(8,128)S(1)}, f32[128,16,128]{0,2,1:T(8,128)S(1)}) fusion(f32[128,16,128]{0,2,1:T(8,128)S(1)} %bitcast.47, f32[16,128,128]{2,1,0:T(8,128)S(1)} %bitcast.49, bf16[128,2048]{1,0:T(8,128)(2,1)} %cq.1), kind=kOutput, calls=%fused_computation.12 | convolution fusion | flops 403437568 | bytes 3678208 | tf_op jit(solution)/shard_map/thd,hde->the/dot_general | solution.py:24
  107.8 0.3 multiply_convert_fusion.1
  108.2 1.0 copy.32
  109.2 1.9 %copy.37 = f32[128,4096]{0,1:T(8,128)S(1)} copy(f32[128,4096]{1,0:T(8,128)} %get-tuple-element.7) | data formatting | bytes 4194304 | tf_op jit(solution)/shard_map/reshape | solution.py:173
  111.1 0.0 copy-start
  111.1 0.0 collective-permute-done
  111.1 1.5 %broadcast_select_fusion.1 = (f32[16,128,128]{1,2,0:T(8,128)S(1)}, f32[16,128,128]{1,2,0:T(8,128)S(1)}) fusion(f32[16,128,128]{1,2,0:T(8,128)S(1)} %copy.28, f32[16,128,128]{1,2,0:T(8,128)} %collective-permute-done, pred[]{:T(512)S(6)} %eq.19), kind=kLoop, calls=%fused_computation.19 | loop fusion | flops 524288 | bytes 4194305 | tf_op jit(solution)/shard_map/jit(_where)/select_n | solution.py:166
  112.6 0.0 copy-done
  112.6 2.3 %multiply_reduce_fusion = (f32[128,32]{0,1:T(8,128)S(1)}, f32[128,32,128]{0,2,1:T(8,128)S(1)}) fusion(f32[128,32,128]{0,2,1:T(8,128)S(1)} %bitcast.46, f32[16,128,128]{1,2,0:T(8,128)S(1)} %get-tuple-element.13, f32[16,128,128]{1,2,0:T(8,128)S(1)} %get-tuple-element.12, bf16[128,4096]{1,0:T(8,128)(2,1)S(1)} %copy-done), kind=kOutput, calls=%fused_computation.6 | convolution fusion | flops 807399424 | bytes 7356416 | tf_op jit(solution)/shard_map/thd,hde->the/dot_general | solution.py:24
  115.0 0.7 multiply_convert_fusion
  115.7 1.3 %copy.33 = bf16[128,4096]{1,0:T(8,128)(2,1)} copy(bf16[128,4096]{0,1:T(8,128)(2,1)S(1)} %bitcast.48) | data formatting | bytes 2097152
  (3 shorter events, 0.0 us)
Async XLA Ops:
  102.5 3.2 %copy-start.1 = (f32[4096]{0:T(1024)S(1)}, f32[4096]{0:T(1024)}, u32[]{:S(2)}) copy-start(f32[4096]{0:T(1024)} %param.15) | copy-start | bytes 49156
  102.9 8.3 %collective-permute-start = (f32[16,128,128]{1,2,0:T(8,128)S(1)}, f32[16,128,128]{1,2,0:T(8,128)}, u32[]{:S(2)}, u32[]{:S(2)}) collective-permute-start(f32[16,128,128]{1,2,0:T(8,128)S(1)} %copy.28), channel_id=1, source_target_pairs={{0,1},{1,0},{2,3},{3,2},{4,5},{5,4},{6,7},{7,6},{8,9},{9,8},{10,11... | collective-permute-start | bytes 3145736 | tf_op jit(solution)/shard_map/ppermute | solution.py:163
  111.1 1.5 %copy-start = (bf16[128,4096]{1,0:T(8,128)(2,1)S(1)}, bf16[128,4096]{1,0:T(8,128)(2,1)}, u32[]{:S(2)}) copy-start(bf16[128,4096]{1,0:T(8,128)(2,1)} %rq.1) | copy-start | bytes 3145732

commit v7 on v6

v7 whole, which is shorter than its diff:
```python
import jax
import jax.numpy as jnp
from jax import lax
from jax.experimental import pallas as pl
from jax.experimental.pallas import tpu as pltpu
from jax.sharding import PartitionSpec as P

DH = 128


def block_state(key, value, heads):
    rows = key.shape[0]
    kh = key.reshape(rows, heads, DH)
    vh = value.reshape(rows, heads, DH)
    return jnp.einsum("shd,she->hde", kh, vh, preferred_element_type=jnp.float32)


def heads_inner(q_ref, k_ref, v_ref, keep, o_ref):
    def one(h, carry):
        cols = pl.ds(pl.multiple_of(h * DH, DH), DH)
        scores = lax.dot_general(
            q_ref[:, cols], k_ref[:, cols], (((1,), (1,)), ((), ())),
            preferred_element_type=jnp.float32,
        )
        scores = jnp.where(keep, scores, 0.0).astype(jnp.bfloat16)
        o_ref[:, cols] = jnp.dot(scores, v_ref[:, cols], preferred_element_type=jnp.float32)
        return carry

    lax.fori_loop(0, q_ref.shape[1] // DH, one, 0)


def split_dot(q, state):
    hi = state.astype(jnp.bfloat16)
    rest = state - hi.astype(jnp.float32)
    mid = rest.astype(jnp.bfloat16)
    lo = (rest - mid.astype(jnp.float32)).astype(jnp.bfloat16)
    acc = jnp.dot(q, hi, preferred_element_type=jnp.float32)
    acc = acc + jnp.dot(q, mid, preferred_element_type=jnp.float32)
    return acc + jnp.dot(q, lo, preferred_element_type=jnp.float32)


def head_state(ref, h, first, half):
    if half <= DH:
        group = DH // half
        return ref[pl.ds(h * group, group), pl.ds(first, half), :].reshape(DH, DH)
    per = half // DH
    return ref[h // per, pl.ds(first + (h % per) * DH, DH), :]


def heads_finish(q_ref, inner_ref, state_of, gain_ref, gain_at, o_ref):
    def one(h, carry):
        cols = pl.ds(pl.multiple_of(h * DH, DH), DH)
        raw = inner_ref[:, cols] + split_dot(q_ref[:, cols], state_of(h))
        square = jnp.mean(raw * raw, axis=-1, keepdims=True)
        gain = gain_ref[:, pl.ds(pl.multiple_of(gain_at + h * DH, DH), DH)]
        o_ref[:, cols] = (raw * lax.rsqrt(square + 1e-06) * gain).astype(o_ref.dtype)
        return carry

    lax.fori_loop(0, q_ref.shape[1] // DH, one, 0)


def layer_kernel(
    x_ref, cq, ck, cv, rq, rk, rv, rmask, gain_ref,
    cat_out, resp_out,
    got, payload, back, whole, cat_inner, resp_inner, sends, recvs,
):
    peers, half = x_ref.shape[0], x_ref.shape[1]
    me = lax.axis_index("seq")
    side = lax.axis_index("resp")
    mesh_ids = pl.DeviceIdType.MESH

    def exchange(phase, src, dst, cover):
        def copy_to(peer, at):
            return pltpu.make_async_remote_copy(
                src_ref=src.at[peer],
                dst_ref=dst.at[at],
                send_sem=sends.at[phase],
                recv_sem=recvs.at[phase],
                device_id={"seq": peer},
                device_id_type=mesh_ids,
            )

        def start(t, carry):
            copy_to(lax.rem(me + t, peers), me).start()
            return carry

        lax.fori_loop(1, peers, start, 0)
        dst[pl.ds(me, 1)] = src[pl.ds(me, 1)]
        cover()
        others = pl.ds(0, peers - 1)
        everyone = pltpu.make_async_remote_copy(
            src_ref=src.at[others],
            dst_ref=dst.at[others],
            send_sem=sends.at[phase],
            recv_sem=recvs.at[phase],
            device_id={"seq": lax.rem(me + 1, peers)},
            device_id_type=mesh_ids,
        )
        everyone.wait_send()
        everyone.wait_recv()

    def cat_cover():
        rows = lax.broadcasted_iota(jnp.int32, (cq.shape[0], cq.shape[0]), 0)
        cols = lax.broadcasted_iota(jnp.int32, (cq.shape[0], cq.shape[0]), 1)
        heads_inner(cq, ck, cv, cols <= rows, cat_inner)

    def resp_cover():
        heads_inner(rq, rk, rv, rmask[...] != 0, resp_inner)

    exchange(0, x_ref, got, cat_cover)

    def running(j, acc):
        payload[pl.ds(j, 1), pl.ds(0, half), :] = acc[None]
        return acc + got[j]

    total = lax.fori_loop(0, peers, running, jnp.zeros((half, DH), jnp.float32), unroll=8)

    def fill(j, carry):
        payload[pl.ds(j, 1), pl.ds(half, half), :] = total[None]
        return carry

    lax.fori_loop(0, peers, fill, 0, unroll=8)
    exchange(1, payload, back, resp_cover)

    partner = pltpu.make_async_remote_copy(
        src_ref=back.at[:, pl.ds(half, half)],
        dst_ref=whole.at[pl.ds(side * peers, peers)],
        send_sem=sends.at[2],
        recv_sem=recvs.at[2],
        device_id={"resp": 1 - side},
        device_id_type=mesh_ids,
    )
    partner.start()
    whole[pl.ds(side * peers, peers)] = back[:, pl.ds(half, half)]

    def prefix_of(h):
        return head_state(back, h, 0, half)

    heads_finish(cq, cat_inner, prefix_of, gain_ref, side * cq.shape[1], cat_out)
    partner.wait_send()
    arrived = pltpu.make_async_remote_copy(
        src_ref=back.at[:, pl.ds(half, half)],
        dst_ref=whole.at[pl.ds((1 - side) * peers, peers)],
        send_sem=sends.at[2],
        recv_sem=recvs.at[2],
        device_id={"resp": 1 - side},
        device_id_type=mesh_ids,
    )
    arrived.wait_recv()

    def total_of(h):
        return head_state(whole, h, 0, half)

    heads_finish(rq, resp_inner, total_of, gain_ref, 0, resp_out)


def layer(local_state, cat, resp, rmask, gain):
    peers = lax.axis_size("seq")
    chunks = local_state.reshape(peers, -1, DH)
    half = chunks.shape[1]
    vmem = pl.BlockSpec(memory_space=pltpu.VMEM)
    cat_rows, cat_width = cat[0].shape
    resp_rows, resp_width = resp[0].shape
    return pl.pallas_call(
        layer_kernel,
        out_shape=(
            jax.ShapeDtypeStruct(cat[0].shape, jnp.bfloat16),
            jax.ShapeDtypeStruct(resp[0].shape, jnp.bfloat16),
        ),
        in_specs=[vmem] * 9,
        out_specs=(vmem, vmem),
        scratch_shapes=[
            pltpu.VMEM((peers, half, DH), jnp.float32),
            pltpu.VMEM((peers, 2 * half, DH), jnp.float32),
            pltpu.VMEM((peers, 2 * half, DH), jnp.float32),
            pltpu.VMEM((2 * peers, half, DH), jnp.float32),
            pltpu.VMEM(cat[0].shape, jnp.float32),
            pltpu.VMEM(resp[0].shape, jnp.float32),
            pltpu.SemaphoreType.DMA((3,)),
            pltpu.SemaphoreType.DMA((3,)),
        ],
        compiler_params=pltpu.CompilerParams(has_side_effects=True),
        cost_estimate=pl.CostEstimate(
            flops=10 * DH * (cat_rows * cat_width + resp_rows * resp_width),
            transcendentals=cat_rows * cat_width // DH + resp_rows * resp_width // DH,
            bytes_accessed=14 * peers * half * DH,
        ),
    )(chunks, *cat, *resp, rmask, gain)


def per_device(
    cat_query, cat_key, cat_value, resp_query, resp_key, resp_value, resp_lengths, norm_gain
):
    heads_here = cat_query.shape[1] // DH
    local_state = block_state(cat_key, cat_value, heads_here)
    rows = jnp.arange(resp_query.shape[0], dtype=jnp.int32)
    ends = jnp.cumsum(resp_lengths[0])
    segment = jnp.sum((rows[:, None] >= ends[None, :]).astype(jnp.int32), axis=1)
    mask = (segment[:, None] == segment[None, :]) & (rows[None, :] <= rows[:, None])
    return layer(
        local_state,
        (cat_query, cat_key, cat_value),
        (resp_query, resp_key, resp_value),
        mask.astype(jnp.int32),
        norm_gain.reshape(1, -1),
    )


def solution(mesh):
    placed = (
        P("seq", "resp"),
        P("seq", "resp"),
        P("seq", "resp"),
        P(("seq", "resp"), None),
        P(("seq", "resp"), None),
        P(("seq", "resp"), None),
        P(("seq", "resp"), None),
        P(),
    )
    return jax.shard_map(
        per_device,
        mesh=mesh,
        in_specs=placed,
        out_specs=(P("seq", "resp"), P(("seq", "resp"), None)),
        check_vma=False,
    )
```

time: 117 us -> 115 us (0.983)
  Pallas kernels: 94.9 us -> 106 us
  matrix products: 6.7 us -> 1.27 us
  local copies, waits for them, and re-layouts: 9.16 us -> 4.96 us
  other arithmetic: 4.19 us -> 0.98 us
  starting transfers between devices: 1.29 us -> 0 us
    pallas_call x1, Pallas kernels: 94.9 us -> 106 us  [layer(): pl.pallas_call(layer_kernel, out_shape=(jax.ShapeDtypeStruct(cat[0].shape...]
    dot_general x2 -> x0, matrix products: 4.39 us -> none  [attend_outer(): jnp.einsum('thd,hde->the', qh, state, precision=lax.Precision.HIGHEST)]
    reshape x3 -> x0, local copies, waits for them, and re-layouts: 3.79 us -> none  [the longest x1 1.91 us: per_device(): resp_inner.reshape(-1, all_heads, DH)]
    slice x1 -> x0, local copies, waits for them, and re-layouts: 1.71 us -> none  [transpose_scan(): total = back[:, half:].reshape(local_state.shape)]
    select_n x1 -> x0, other arithmetic: 1.49 us -> none  [per_device(): jnp.where(first, total, other)]
    ppermute x1 -> x0, starting transfers between devices: 1.29 us -> none  [per_device(): other = lax.ppermute(total, 'resp', [(0, 1), (1, 0)])]
    unnamed x6 -> x8, local copies, waits for them, and re-layouts: 2.35 us -> 3.6 us
  transfers between devices with their start and end apart: 1 -> 0, of which waited for: 0 -> 0; matrix products, arithmetic and copies ran while one was open for 6% -> 0% of each run, Pallas kernels for 0% -> 0%
where the time goes in v7:
time: 115 us; the launch traced here: 114 us
  Pallas kernels  106 us (92%)
  local copies, waits for them, and re-layouts  4.96 us (4%)
  matrix products  1.27 us (1%)
    pallas_call x1, Pallas kernels, layer(): pl.pallas_call(layer_kernel, out_shape=(jax.ShapeDtypeStruct(cat[0].shape...  106 us
    unnamed x8, local copies, waits for them, and re-layouts  3.6 us

profile of v7, /device:TPU:1, one launch (start us, length us, event | category | flops | bytes accessed | tf_op | source)
XLA Modules:
  0.0 114.4 jit_solution(5066410251507192986)
XLA Ops:
  0.6 0.0 copy-start.2
  0.6 0.6 copy-done.2
  1.3 0.2 reduce-window.8
  1.5 0.1 convert_reduce_fusion
  1.6 0.7 fusion.4.rmask
  2.3 0.0 copy-start
  2.3 1.4 %copy.14 = bf16[128,2048]{0,1:T(8,128)(2,1)S(1)} copy(bf16[128,2048]{1,0:T(8,128)(2,1)} %ck.1) | data formatting | bytes 1048576 | tf_op jit(solution)/shard_map/reshape | solution.py:13
  3.6 0.0 copy-done
  3.7 1.3 %fusion = f32[16,128,128]{2,1,0:T(8,128)} fusion(bf16[128,16,128]{0,2,1:T(8,128)(2,1)S(1)} %bitcast.14, bf16[128,2048]{1,0:T(8,128)(2,1)S(1)} %copy-done), kind=kOutput, calls=%fused_computation | convolution fusion | flops 67108864 | bytes 2097152 | tf_op jit(solution)/shard_map/shd,she->hde/dot_general | solution.py:15
  4.9 106.5 %shard_map.95 = (bf16[128,2048]{1,0:T(8,128)(2,1)}, bf16[128,4096]{1,0:T(8,128)(2,1)}) custom-call(f32[128,16,128]{2,1,0:T(8,128)} %bitcast.13, bf16[128,2048]{1,0:T(8,128)(2,1)} %cq.1, bf16[128,2048]{1,0:T(8,128)(2,1)} %ck.1, bf16[128,2048]{1,0:T(8,128)(2,1)} %cv.1, bf16[128,4096]{1,0:T(8,128)(2,1)} %rq.1, bf16[128,4096]{1,0:T(8,128)(2,1)} %rk.1, ...), custom_call_target="tpu_custom_call" | custom-call | flops 1006632960 | bytes 3670016 | tf_op jit(solution)/shard_map/pallas_call | solution.py:164
  111.4 0.0 copy-start.1
  111.4 2.0 %copy.22 = bf16[128,2048]{1,0:T(8,128)(2,1)} copy(bf16[128,2048]{1,0:T(8,128)(2,1)} %get-tuple-element.4) | data formatting | bytes 1048576
  113.4 0.0 copy-done.1
  113.4 1.0 copy.23
Async XLA Ops:
  0.6 0.7 copy-start.2
  2.3 1.4 %copy-start = (bf16[128,2048]{1,0:T(8,128)(2,1)S(1)}, bf16[128,2048]{1,0:T(8,128)(2,1)}, u32[]{:S(2)}) copy-start(bf16[128,2048]{1,0:T(8,128)(2,1)} %cv.1) | copy-start | bytes 1572868
  111.4 2.0 %copy-start.1 = (bf16[128,4096]{1,0:T(8,128)(2,1)S(1)}, bf16[128,4096]{1,0:T(8,128)(2,1)}, u32[]{:S(2)}) copy-start(bf16[128,4096]{1,0:T(8,128)(2,1)} %get-tuple-element.5) | copy-start | bytes 3145732

commit v8 on v7

--- a/solution.py
+++ b/solution.py
@@ -6,6 +6,7 @@
 from jax.sharding import PartitionSpec as P
 
 DH = 128
+UNROLL = 4
 
 
 def block_state(key, value, heads):
@@ -26,7 +27,7 @@
         o_ref[:, cols] = jnp.dot(scores, v_ref[:, cols], preferred_element_type=jnp.float32)
         return carry
 
-    lax.fori_loop(0, q_ref.shape[1] // DH, one, 0)
+    lax.fori_loop(0, q_ref.shape[1] // DH, one, 0, unroll=UNROLL)
 
 
 def split_dot(q, state):
@@ -56,7 +57,7 @@
         o_ref[:, cols] = (raw * lax.rsqrt(square + 1e-06) * gain).astype(o_ref.dtype)
         return carry
 
-    lax.fori_loop(0, q_ref.shape[1] // DH, one, 0)
+    lax.fori_loop(0, q_ref.shape[1] // DH, one, 0, unroll=UNROLL)
 
 
 def layer_kernel(

time: 115 us -> 108 us (0.939)
  Pallas kernels: 106 us -> 100 us
    pallas_call x1, Pallas kernels: 106 us -> 100 us  [layer(): pl.pallas_call(layer_kernel, out_shape=(jax.ShapeDtypeStruct(cat[0].shape...]
where the time goes in v8:
time: 108 us
  Pallas kernels  100 us (93%)
  local copies, waits for them, and re-layouts  4.96 us (5%)
  matrix products  1.27 us (1%)
    pallas_call x1, Pallas kernels, layer(): pl.pallas_call(layer_kernel, out_shape=(jax.ShapeDtypeStruct(cat[0].shape...  100 us
    unnamed x8, local copies, waits for them, and re-layouts  3.6 us

profile of v8, /device:TPU:1, one launch (start us, length us, event | category | flops | bytes accessed | tf_op | source)
XLA Modules:
  0.0 108.0 jit_solution(17810052787579659877)
XLA Ops:
  0.6 0.0 copy-start.2
  0.6 0.6 copy-done.2
  1.3 0.2 reduce-window.8
  1.5 0.1 convert_reduce_fusion
  1.6 0.7 fusion.4.rmask
  2.3 0.0 copy-start
  2.3 1.4 %copy.14 = bf16[128,2048]{0,1:T(8,128)(2,1)S(1)} copy(bf16[128,2048]{1,0:T(8,128)(2,1)} %ck.1) | data formatting | bytes 1048576 | tf_op jit(solution)/shard_map/reshape | solution.py:14
  3.6 0.0 copy-done
  3.7 1.3 %fusion = f32[16,128,128]{2,1,0:T(8,128)} fusion(bf16[128,16,128]{0,2,1:T(8,128)(2,1)S(1)} %bitcast.14, bf16[128,2048]{1,0:T(8,128)(2,1)S(1)} %copy-done), kind=kOutput, calls=%fused_computation | convolution fusion | flops 67108864 | bytes 2097152 | tf_op jit(solution)/shard_map/shd,she->hde/dot_general | solution.py:16
  4.9 100.1 %shard_map.95 = (bf16[128,2048]{1,0:T(8,128)(2,1)}, bf16[128,4096]{1,0:T(8,128)(2,1)}) custom-call(f32[128,16,128]{2,1,0:T(8,128)} %bitcast.13, bf16[128,2048]{1,0:T(8,128)(2,1)} %cq.1, bf16[128,2048]{1,0:T(8,128)(2,1)} %ck.1, bf16[128,2048]{1,0:T(8,128)(2,1)} %cv.1, bf16[128,4096]{1,0:T(8,128)(2,1)} %rq.1, bf16[128,4096]{1,0:T(8,128)(2,1)} %rk.1, ...), custom_call_target="tpu_custom_call" | custom-call | flops 1006632960 | bytes 3670016 | tf_op jit(solution)/shard_map/pallas_call | solution.py:165
  105.1 0.0 copy-start.1
  105.1 2.0 %copy.22 = bf16[128,2048]{1,0:T(8,128)(2,1)} copy(bf16[128,2048]{1,0:T(8,128)(2,1)} %get-tuple-element.4) | data formatting | bytes 1048576
  107.0 0.0 copy-done.1
  107.0 1.0 copy.23
Async XLA Ops:
  0.6 0.7 copy-start.2
  2.3 1.4 %copy-start = (bf16[128,2048]{1,0:T(8,128)(2,1)S(1)}, bf16[128,2048]{1,0:T(8,128)(2,1)}, u32[]{:S(2)}) copy-start(bf16[128,2048]{1,0:T(8,128)(2,1)} %cv.1) | copy-start | bytes 1572868
  105.1 2.0 %copy-start.1 = (bf16[128,4096]{1,0:T(8,128)(2,1)S(1)}, bf16[128,4096]{1,0:T(8,128)(2,1)}, u32[]{:S(2)}) copy-start(bf16[128,4096]{1,0:T(8,128)(2,1)} %get-tuple-element.5) | copy-start | bytes 3145732

commit v9 on v8

--- a/solution.py
+++ b/solution.py
@@ -48,49 +48,48 @@
     return ref[h // per, pl.ds(first + (h % per) * DH, DH), :]
 
 
-def heads_finish(q_ref, inner_ref, state_of, gain_ref, gain_at, o_ref):
-    def one(h, carry):
-        cols = pl.ds(pl.multiple_of(h * DH, DH), DH)
-        raw = inner_ref[:, cols] + split_dot(q_ref[:, cols], state_of(h))
+def heads_finish(q_ref, inner_ref, state_of, gain_ref, gain_at, first, count, o_ref):
+    def one(i, carry):
+        cols = pl.ds(pl.multiple_of((first + i) * DH, DH), DH)
+        raw = inner_ref[:, cols] + split_dot(q_ref[:, cols], state_of(i))
         square = jnp.mean(raw * raw, axis=-1, keepdims=True)
-        gain = gain_ref[:, pl.ds(pl.multiple_of(gain_at + h * DH, DH), DH)]
+        gain = gain_ref[:, pl.ds(pl.multiple_of(gain_at + (first + i) * DH, DH), DH)]
         o_ref[:, cols] = (raw * lax.rsqrt(square + 1e-06) * gain).astype(o_ref.dtype)
         return carry
 
-    lax.fori_loop(0, q_ref.shape[1] // DH, one, 0, unroll=UNROLL)
+    lax.fori_loop(0, count, one, 0, unroll=UNROLL)
 
 
 def layer_kernel(
     x_ref, cq, ck, cv, rq, rk, rv, rmask, gain_ref,
     cat_out, resp_out,
-    got, payload, back, whole, cat_inner, resp_inner, sends, recvs,
+    got, payload, total_ref, before, totals, partner_totals, cat_inner, resp_inner, sends, recvs,
 ):
     peers, half = x_ref.shape[0], x_ref.shape[1]
+    heads_here = cq.shape[1] // DH
     me = lax.axis_index("seq")
     side = lax.axis_index("resp")
     mesh_ids = pl.DeviceIdType.MESH
 
-    def exchange(phase, src, dst, cover):
-        def copy_to(peer, at):
-            return pltpu.make_async_remote_copy(
-                src_ref=src.at[peer],
-                dst_ref=dst.at[at],
+    def start_all(phase, src_of, dst):
+        def start(t, carry):
+            peer = lax.rem(me + t, peers)
+            pltpu.make_async_remote_copy(
+                src_ref=src_of(peer),
+                dst_ref=dst.at[me],
                 send_sem=sends.at[phase],
                 recv_sem=recvs.at[phase],
                 device_id={"seq": peer},
                 device_id_type=mesh_ids,
-            )
-
-        def start(t, carry):
-            copy_to(lax.rem(me + t, peers), me).start()
+            ).start()
             return carry
 
         lax.fori_loop(1, peers, start, 0)
-        dst[pl.ds(me, 1)] = src[pl.ds(me, 1)]
-        cover()
+
+    def wait_all(phase, dst):
         others = pl.ds(0, peers - 1)
         everyone = pltpu.make_async_remote_copy(
-            src_ref=src.at[others],
+            src_ref=dst.at[others],
             dst_ref=dst.at[others],
             send_sem=sends.at[phase],
             recv_sem=recvs.at[phase],
@@ -100,59 +99,51 @@
         everyone.wait_send()
         everyone.wait_recv()
 
-    def cat_cover():
-        rows = lax.broadcasted_iota(jnp.int32, (cq.shape[0], cq.shape[0]), 0)
-        cols = lax.broadcasted_iota(jnp.int32, (cq.shape[0], cq.shape[0]), 1)
-        heads_inner(cq, ck, cv, cols <= rows, cat_inner)
-
-    def resp_cover():
-        heads_inner(rq, rk, rv, rmask[...] != 0, resp_inner)
-
-    exchange(0, x_ref, got, cat_cover)
+    start_all(0, lambda peer: x_ref.at[peer], got)
+    got[pl.ds(me, 1)] = x_ref[pl.ds(me, 1)]
+    rows = lax.broadcasted_iota(jnp.int32, (cq.shape[0], cq.shape[0]), 0)
+    cols = lax.broadcasted_iota(jnp.int32, (cq.shape[0], cq.shape[0]), 1)
+    heads_inner(cq, ck, cv, cols <= rows, cat_inner)
+    wait_all(0, got)
 
     def running(j, acc):
-        payload[pl.ds(j, 1), pl.ds(0, half), :] = acc[None]
+        payload[pl.ds(j, 1)] = acc[None]
         return acc + got[j]
 
-    total = lax.fori_loop(0, peers, running, jnp.zeros((half, DH), jnp.float32), unroll=8)
-
-    def fill(j, carry):
-        payload[pl.ds(j, 1), pl.ds(half, half), :] = total[None]
-        return carry
-
-    lax.fori_loop(0, peers, fill, 0, unroll=8)
-    exchange(1, payload, back, resp_cover)
-
+    total_ref[...] = lax.fori_loop(
+        0, peers, running, jnp.zeros((half, DH), jnp.float32), unroll=8
+    )[None]
+    start_all(1, lambda peer: payload.at[peer], before)
+    start_all(2, lambda peer: total_ref.at[0], totals)
+    before[pl.ds(me, 1)] = payload[pl.ds(me, 1)]
+    totals[pl.ds(me, 1)] = total_ref[...]
+    heads_inner(rq, rk, rv, rmask[...] != 0, resp_inner)
+
+    wait_all(1, before)
+    heads_finish(
+        cq, cat_inner, lambda i: head_state(before, i, 0, half), gain_ref,
+        side * cq.shape[1], 0, heads_here, cat_out,
+    )
+    wait_all(2, totals)
     partner = pltpu.make_async_remote_copy(
-        src_ref=back.at[:, pl.ds(half, half)],
-        dst_ref=whole.at[pl.ds(side * peers, peers)],
-        send_sem=sends.at[2],
-        recv_sem=recvs.at[2],
+        src_ref=totals,
+        dst_ref=partner_totals,
+        send_sem=sends.at[3],
+        recv_sem=recvs.at[3],
         device_id={"resp": 1 - side},
         device_id_type=mesh_ids,
     )
     partner.start()
-    whole[pl.ds(side * peers, peers)] = back[:, pl.ds(half, half)]
-
-    def prefix_of(h):
-        return head_state(back, h, 0, half)
-
-    heads_finish(cq, cat_inner, prefix_of, gain_ref, side * cq.shape[1], cat_out)
+    heads_finish(
+        rq, resp_inner, lambda i: head_state(totals, i, 0, half), gain_ref,
+        0, side * heads_here, heads_here, resp_out,
+    )
     partner.wait_send()
-    arrived = pltpu.make_async_remote_copy(
-        src_ref=back.at[:, pl.ds(half, half)],
-        dst_ref=whole.at[pl.ds((1 - side) * peers, peers)],
-        send_sem=sends.at[2],
-        recv_sem=recvs.at[2],
-        device_id={"resp": 1 - side},
-        device_id_type=mesh_ids,
-    )
-    arrived.wait_recv()
-
-    def total_of(h):
-        return head_state(whole, h, 0, half)
-
-    heads_finish(rq, resp_inner, total_of, gain_ref, 0, resp_out)
+    partner.wait_recv()
+    heads_finish(
+        rq, resp_inner, lambda i: head_state(partner_totals, i, 0, half), gain_ref,
+        0, (1 - side) * heads_here, heads_here, resp_out,
+    )
 
 
 def layer(local_state, cat, resp, rmask, gain):
@@ -172,13 +163,15 @@
         out_specs=(vmem, vmem),
         scratch_shapes=[
             pltpu.VMEM((peers, half, DH), jnp.float32),
-            pltpu.VMEM((peers, 2 * half, DH), jnp.float32),
-            pltpu.VMEM((peers, 2 * half, DH), jnp.float32),
-            pltpu.VMEM((2 * peers, half, DH), jnp.float32),
+            pltpu.VMEM((peers, half, DH), jnp.float32),
+            pltpu.VMEM((1, half, DH), jnp.float32),
+            pltpu.VMEM((peers, half, DH), jnp.float32),
+            pltpu.VMEM((peers, half, DH), jnp.float32),
+            pltpu.VMEM((peers, half, DH), jnp.float32),
             pltpu.VMEM(cat[0].shape, jnp.float32),
             pltpu.VMEM(resp[0].shape, jnp.float32),
-            pltpu.SemaphoreType.DMA((3,)),
-            pltpu.SemaphoreType.DMA((3,)),
+            pltpu.SemaphoreType.DMA((4,)),
+            pltpu.SemaphoreType.DMA((4,)),
         ],
         compiler_params=pltpu.CompilerParams(has_side_effects=True),
         cost_estimate=pl.CostEstimate(

time: 108 us -> 107 us (level)
  Pallas kernels: 100 us -> 98.7 us
    pallas_call x1, Pallas kernels: 100 us -> 98.7 us  [layer(): pl.pallas_call(layer_kernel, out_shape=(jax.ShapeDtypeStruct(cat[0].shape...]
where the time goes in v9:
time: 107 us
  Pallas kernels  98.7 us (92%)
  local copies, waits for them, and re-layouts  4.96 us (5%)
  matrix products  1.27 us (1%)
    pallas_call x1, Pallas kernels, layer(): pl.pallas_call(layer_kernel, out_shape=(jax.ShapeDtypeStruct(cat[0].shape...  98.7 us
    unnamed x8, local copies, waits for them, and re-layouts  3.6 us

profile of v9, /device:TPU:1, one launch (start us, length us, event | category | flops | bytes accessed | tf_op | source)
XLA Modules:
  0.0 106.6 jit_solution(18267905251598250861)
XLA Ops:
  0.6 0.0 copy-start.2
  0.6 0.6 copy-done.2
  1.3 0.2 reduce-window.8
  1.5 0.1 convert_reduce_fusion
  1.6 0.7 fusion.4.rmask
  2.3 0.0 copy-start
  2.3 1.4 %copy.14 = bf16[128,2048]{0,1:T(8,128)(2,1)S(1)} copy(bf16[128,2048]{1,0:T(8,128)(2,1)} %ck.1) | data formatting | bytes 1048576 | tf_op jit(solution)/shard_map/reshape | solution.py:14
  3.6 0.0 copy-done
  3.7 1.3 %fusion = f32[16,128,128]{2,1,0:T(8,128)} fusion(bf16[128,16,128]{0,2,1:T(8,128)(2,1)S(1)} %bitcast.14, bf16[128,2048]{1,0:T(8,128)(2,1)S(1)} %copy-done), kind=kOutput, calls=%fused_computation | convolution fusion | flops 67108864 | bytes 2097152 | tf_op jit(solution)/shard_map/shd,she->hde/dot_general | solution.py:16
  4.9 98.7 %shard_map.95 = (bf16[128,2048]{1,0:T(8,128)(2,1)}, bf16[128,4096]{1,0:T(8,128)(2,1)}) custom-call(f32[128,16,128]{2,1,0:T(8,128)} %bitcast.13, bf16[128,2048]{1,0:T(8,128)(2,1)} %cq.1, bf16[128,2048]{1,0:T(8,128)(2,1)} %ck.1, bf16[128,2048]{1,0:T(8,128)(2,1)} %cv.1, bf16[128,4096]{1,0:T(8,128)(2,1)} %rq.1, bf16[128,4096]{1,0:T(8,128)(2,1)} %rk.1, ...), custom_call_target="tpu_custom_call" | custom-call | flops 1006632960 | bytes 3670016 | tf_op jit(solution)/shard_map/pallas_call | solution.py:156
  103.6 0.0 copy-start.1
  103.6 2.0 %copy.22 = bf16[128,2048]{1,0:T(8,128)(2,1)} copy(bf16[128,2048]{1,0:T(8,128)(2,1)} %get-tuple-element.4) | data formatting | bytes 1048576
  105.6 0.0 copy-done.1
  105.6 1.0 copy.23
Async XLA Ops:
  0.6 0.7 copy-start.2
  2.3 1.4 %copy-start = (bf16[128,2048]{1,0:T(8,128)(2,1)S(1)}, bf16[128,2048]{1,0:T(8,128)(2,1)}, u32[]{:S(2)}) copy-start(bf16[128,2048]{1,0:T(8,128)(2,1)} %cv.1) | copy-start | bytes 1572868
  103.6 2.0 %copy-start.1 = (bf16[128,4096]{1,0:T(8,128)(2,1)S(1)}, bf16[128,4096]{1,0:T(8,128)(2,1)}, u32[]{:S(2)}) copy-start(bf16[128,4096]{1,0:T(8,128)(2,1)} %get-tuple-element.5) | copy-start | bytes 3145732

commit v10 on v9

--- a/solution.py
+++ b/solution.py
@@ -6,7 +6,7 @@
 from jax.sharding import PartitionSpec as P
 
 DH = 128
-UNROLL = 4
+UNROLL = 8
 
 
 def block_state(key, value, heads):
@@ -48,6 +48,15 @@
     return ref[h // per, pl.ds(first + (h % per) * DH, DH), :]
 
 
+def put_head_state(ref, h, value, half):
+    if half <= DH:
+        group = DH // half
+        ref[pl.ds(h * group, group)] = value.reshape(group, half, DH)
+    else:
+        per = half // DH
+        ref[h // per, pl.ds((h % per) * DH, DH), :] = value
+
+
 def heads_finish(q_ref, inner_ref, state_of, gain_ref, gain_at, first, count, o_ref):
     def one(i, carry):
         cols = pl.ds(pl.multiple_of((first + i) * DH, DH), DH)
@@ -61,12 +70,24 @@
 
 
 def layer_kernel(
-    x_ref, cq, ck, cv, rq, rk, rv, rmask, gain_ref,
+    cq, ck, cv, rq, rk, rv, lengths, gain_ref,
     cat_out, resp_out,
-    got, payload, total_ref, before, totals, partner_totals, cat_inner, resp_inner, sends, recvs,
+    x_ref, got, payload, total_ref, before, totals, partner_totals, cat_inner, resp_inner,
+    sends, recvs,
 ):
     peers, half = x_ref.shape[0], x_ref.shape[1]
     heads_here = cq.shape[1] // DH
+
+    def own_state(h, carry):
+        cols = pl.ds(pl.multiple_of(h * DH, DH), DH)
+        value = lax.dot_general(
+            ck[:, cols], cv[:, cols], (((0,), (0,)), ((), ())),
+            preferred_element_type=jnp.float32,
+        )
+        put_head_state(x_ref, h, value, half)
+        return carry
+
+    lax.fori_loop(0, heads_here, own_state, 0, unroll=UNROLL)
     me = lax.axis_index("seq")
     side = lax.axis_index("resp")
     mesh_ids = pl.DeviceIdType.MESH
@@ -117,7 +138,16 @@
     start_all(2, lambda peer: total_ref.at[0], totals)
     before[pl.ds(me, 1)] = payload[pl.ds(me, 1)]
     totals[pl.ds(me, 1)] = total_ref[...]
-    heads_inner(rq, rk, rv, rmask[...] != 0, resp_inner)
+    rrows = lax.broadcasted_iota(jnp.int32, (rq.shape[0], rq.shape[0]), 0)
+    rcols = lax.broadcasted_iota(jnp.int32, (rq.shape[0], rq.shape[0]), 1)
+    end = lengths[0, 0]
+    row_seg = (rrows >= end).astype(jnp.int32)
+    col_seg = (rcols >= end).astype(jnp.int32)
+    for k in range(1, lengths.shape[1]):
+        end = end + lengths[0, k]
+        row_seg = row_seg + (rrows >= end).astype(jnp.int32)
+        col_seg = col_seg + (rcols >= end).astype(jnp.int32)
+    heads_inner(rq, rk, rv, (row_seg == col_seg) & (rcols <= rrows), resp_inner)
 
     wait_all(1, before)
     heads_finish(
@@ -146,10 +176,9 @@
     )
 
 
-def layer(local_state, cat, resp, rmask, gain):
+def layer(cat, resp, lengths, gain):
     peers = lax.axis_size("seq")
-    chunks = local_state.reshape(peers, -1, DH)
-    half = chunks.shape[1]
+    half = cat[0].shape[1] // peers
     vmem = pl.BlockSpec(memory_space=pltpu.VMEM)
     cat_rows, cat_width = cat[0].shape
     resp_rows, resp_width = resp[0].shape
@@ -159,9 +188,10 @@
             jax.ShapeDtypeStruct(cat[0].shape, jnp.bfloat16),
             jax.ShapeDtypeStruct(resp[0].shape, jnp.bfloat16),
         ),
-        in_specs=[vmem] * 9,
+        in_specs=[vmem] * 6 + [pl.BlockSpec(memory_space=pltpu.SMEM), vmem],
         out_specs=(vmem, vmem),
         scratch_shapes=[
+            pltpu.VMEM((peers, half, DH), jnp.float32),
             pltpu.VMEM((peers, half, DH), jnp.float32),
             pltpu.VMEM((peers, half, DH), jnp.float32),
             pltpu.VMEM((1, half, DH), jnp.float32),
@@ -179,23 +209,16 @@
             transcendentals=cat_rows * cat_width // DH + resp_rows * resp_width // DH,
             bytes_accessed=14 * peers * half * DH,
         ),
-    )(chunks, *cat, *resp, rmask, gain)
+    )(*cat, *resp, lengths, gain)
 
 
 def per_device(
     cat_query, cat_key, cat_value, resp_query, resp_key, resp_value, resp_lengths, norm_gain
 ):
-    heads_here = cat_query.shape[1] // DH
-    local_state = block_state(cat_key, cat_value, heads_here)
-    rows = jnp.arange(resp_query.shape[0], dtype=jnp.int32)
-    ends = jnp.cumsum(resp_lengths[0])
-    segment = jnp.sum((rows[:, None] >= ends[None, :]).astype(jnp.int32), axis=1)
-    mask = (segment[:, None] == segment[None, :]) & (rows[None, :] <= rows[:, None])
     return layer(
-        local_state,
         (cat_query, cat_key, cat_value),
         (resp_query, resp_key, resp_value),
-        mask.astype(jnp.int32),
+        resp_lengths,
         norm_gain.reshape(1, -1),
     )
 

time: 107 us -> 102 us (0.953)
  local copies, waits for them, and re-layouts: 4.96 us -> 2.94 us
  matrix products: 1.27 us -> 0 us
    reshape x1 -> x0, local copies, waits for them, and re-layouts: 1.37 us -> none  [block_state(): kh = key.reshape(rows, heads, DH)]
    dot_general x1 -> x0, matrix products: 1.27 us -> none  [block_state(): jnp.einsum('shd,she->hde', kh, vh, preferred_element_type=jnp.float32)]
    unnamed x8 -> x4, local copies, waits for them, and re-layouts: 3.6 us -> 2.94 us
where the time goes in v10:
time: 102 us
  Pallas kernels  98.6 us (97%)
  local copies, waits for them, and re-layouts  2.94 us (3%)
    pallas_call x1, Pallas kernels, layer(): pl.pallas_call(layer_kernel, out_shape=(jax.ShapeDtypeStruct(cat[0].shape...  98.6 us
    unnamed x4, local copies, waits for them, and re-layouts  2.94 us

profile of v10, /device:TPU:1, one launch (start us, length us, event | category | flops | bytes accessed | tf_op | source)
XLA Modules:
  0.0 102.2 jit_solution(11466987325008974073)
XLA Ops:
  0.6 98.6 %shard_map.95 = (bf16[128,2048]{1,0:T(8,128)(2,1)}, bf16[128,4096]{1,0:T(8,128)(2,1)}) custom-call(bf16[128,2048]{1,0:T(8,128)(2,1)} %cq.1, bf16[128,2048]{1,0:T(8,128)(2,1)} %ck.1, bf16[128,2048]{1,0:T(8,128)(2,1)} %cv.1, bf16[128,4096]{1,0:T(8,128)(2,1)} %rq.1, bf16[128,4096]{1,0:T(8,128)(2,1)} %rk.1, bf16[128,4096]{1,0:T(8,128)(2,1)} %rv.1, ...), custom_call_target="tpu_custom_call" | custom-call | flops 1006632960 | bytes 3670016 | tf_op jit(solution)/shard_map/pallas_call | solution.py:185
  99.2 0.0 copy-start
  99.2 2.0 %copy.12 = bf16[128,2048]{1,0:T(8,128)(2,1)} copy(bf16[128,2048]{1,0:T(8,128)(2,1)} %get-tuple-element.4) | data formatting | bytes 1048576
  101.2 0.0 copy-done
  101.2 1.0 copy.13
Async XLA Ops:
  99.2 2.0 %copy-start = (bf16[128,4096]{1,0:T(8,128)(2,1)S(1)}, bf16[128,4096]{1,0:T(8,128)(2,1)}, u32[]{:S(2)}) copy-start(bf16[128,4096]{1,0:T(8,128)(2,1)} %get-tuple-element.5) | copy-start | bytes 3145732

commit v11 on v10

--- a/solution.py
+++ b/solution.py
@@ -77,6 +77,19 @@
 ):
     peers, half = x_ref.shape[0], x_ref.shape[1]
     heads_here = cq.shape[1] // DH
+    me = lax.axis_index("seq")
+    side = lax.axis_index("resp")
+    mesh_ids = pl.DeviceIdType.MESH
+    barrier = pltpu.get_barrier_semaphore()
+
+    def greet(t, carry):
+        pl.semaphore_signal(
+            barrier, 1, device_id={"seq": lax.rem(me + t, peers)}, device_id_type=mesh_ids
+        )
+        return carry
+
+    lax.fori_loop(1, peers, greet, 0)
+    pl.semaphore_signal(barrier, 1, device_id={"resp": 1 - side}, device_id_type=mesh_ids)
 
     def own_state(h, carry):
         cols = pl.ds(pl.multiple_of(h * DH, DH), DH)
@@ -88,9 +101,7 @@
         return carry
 
     lax.fori_loop(0, heads_here, own_state, 0, unroll=UNROLL)
-    me = lax.axis_index("seq")
-    side = lax.axis_index("resp")
-    mesh_ids = pl.DeviceIdType.MESH
+    pl.semaphore_wait(barrier, peers)
 
     def start_all(phase, src_of, dst):
         def start(t, carry):
@@ -203,7 +214,7 @@
             pltpu.SemaphoreType.DMA((4,)),
             pltpu.SemaphoreType.DMA((4,)),
         ],
-        compiler_params=pltpu.CompilerParams(has_side_effects=True),
+        compiler_params=pltpu.CompilerParams(collective_id=0, has_side_effects=True),
         cost_estimate=pl.CostEstimate(
             flops=10 * DH * (cat_rows * cat_width + resp_rows * resp_width),
             transcendentals=cat_rows * cat_width // DH + resp_rows * resp_width // DH,

time: 102 us -> 98.3 us (0.964)
  Pallas kernels: 98.6 us -> 94.6 us
    pallas_call x1, Pallas kernels: 98.6 us -> 94.6 us  [layer(): pl.pallas_call(layer_kernel, out_shape=(jax.ShapeDtypeStruct(cat[0].shape...]
where the time goes in v11:
time: 98.3 us; the launch traced here: 98.2 us
  Pallas kernels  94.6 us (96%)
  local copies, waits for them, and re-layouts  2.94 us (3%)
    pallas_call x1, Pallas kernels, layer(): pl.pallas_call(layer_kernel, out_shape=(jax.ShapeDtypeStruct(cat[0].shape...  94.6 us
    unnamed x4, local copies, waits for them, and re-layouts  2.94 us

profile of v11, /device:TPU:1, one launch (start us, length us, event | category | flops | bytes accessed | tf_op | source)
XLA Modules:
  0.0 98.2 jit_solution(5433472572530437608)
XLA Ops:
  0.6 94.6 %shard_map.95 = (bf16[128,2048]{1,0:T(8,128)(2,1)}, bf16[128,4096]{1,0:T(8,128)(2,1)}) custom-call(bf16[128,2048]{1,0:T(8,128)(2,1)} %cq.1, bf16[128,2048]{1,0:T(8,128)(2,1)} %ck.1, bf16[128,2048]{1,0:T(8,128)(2,1)} %cv.1, bf16[128,4096]{1,0:T(8,128)(2,1)} %rq.1, bf16[128,4096]{1,0:T(8,128)(2,1)} %rk.1, bf16[128,4096]{1,0:T(8,128)(2,1)} %rv.1, ...), custom_call_target="tpu_custom_call" | custom-call | flops 1006632960 | bytes 3670016 | tf_op jit(solution)/shard_map/pallas_call | solution.py:196
  95.2 0.0 copy-start
  95.3 2.0 %copy.12 = bf16[128,2048]{1,0:T(8,128)(2,1)} copy(bf16[128,2048]{1,0:T(8,128)(2,1)} %get-tuple-element.4) | data formatting | bytes 1048576
  97.2 0.0 copy-done
  97.2 1.0 copy.13
Async XLA Ops:
  95.2 2.0 %copy-start = (bf16[128,4096]{1,0:T(8,128)(2,1)S(1)}, bf16[128,4096]{1,0:T(8,128)(2,1)}, u32[]{:S(2)}) copy-start(bf16[128,4096]{1,0:T(8,128)(2,1)} %get-tuple-element.5) | copy-start | bytes 3145732

commit v12 on v11

--- a/solution.py
+++ b/solution.py
@@ -103,12 +103,14 @@
     lax.fori_loop(0, heads_here, own_state, 0, unroll=UNROLL)
     pl.semaphore_wait(barrier, peers)
 
-    def start_all(phase, src_of, dst):
+    part = half // 2
+
+    def start_all(phase, src_of, dst, k):
         def start(t, carry):
             peer = lax.rem(me + t, peers)
             pltpu.make_async_remote_copy(
                 src_ref=src_of(peer),
-                dst_ref=dst.at[me],
+                dst_ref=dst.at[me, pl.ds(k * part, part)],
                 send_sem=sends.at[phase],
                 recv_sem=recvs.at[phase],
                 device_id={"seq": peer},
@@ -118,11 +120,11 @@
 
         lax.fori_loop(1, peers, start, 0)
 
-    def wait_all(phase, dst):
+    def wait_all(phase, dst, k):
         others = pl.ds(0, peers - 1)
         everyone = pltpu.make_async_remote_copy(
-            src_ref=dst.at[others],
-            dst_ref=dst.at[others],
+            src_ref=dst.at[others, pl.ds(k * part, part)],
+            dst_ref=dst.at[others, pl.ds(k * part, part)],
             send_sem=sends.at[phase],
             recv_sem=recvs.at[phase],
             device_id={"seq": lax.rem(me + 1, peers)},
@@ -131,22 +133,26 @@
         everyone.wait_send()
         everyone.wait_recv()
 
-    start_all(0, lambda peer: x_ref.at[peer], got)
+    for k in range(2):
+        start_all(k, lambda peer, k=k: x_ref.at[peer, pl.ds(k * part, part)], got, k)
     got[pl.ds(me, 1)] = x_ref[pl.ds(me, 1)]
     rows = lax.broadcasted_iota(jnp.int32, (cq.shape[0], cq.shape[0]), 0)
     cols = lax.broadcasted_iota(jnp.int32, (cq.shape[0], cq.shape[0]), 1)
     heads_inner(cq, ck, cv, cols <= rows, cat_inner)
-    wait_all(0, got)
-
-    def running(j, acc):
-        payload[pl.ds(j, 1)] = acc[None]
-        return acc + got[j]
-
-    total_ref[...] = lax.fori_loop(
-        0, peers, running, jnp.zeros((half, DH), jnp.float32), unroll=8
-    )[None]
-    start_all(1, lambda peer: payload.at[peer], before)
-    start_all(2, lambda peer: total_ref.at[0], totals)
+
+    for k in range(2):
+        wait_all(k, got, k)
+        rows_k = pl.ds(k * part, part)
+
+        def running(j, acc, rows_k=rows_k):
+            payload[pl.ds(j, 1), rows_k] = acc[None]
+            return acc + got[j, rows_k]
+
+        total_ref[:, rows_k] = lax.fori_loop(
+            0, peers, running, jnp.zeros((part, DH), jnp.float32), unroll=8
+        )[None]
+        start_all(2 + k, lambda peer, rows_k=rows_k: payload.at[peer, rows_k], before, k)
+        start_all(4 + k, lambda peer, rows_k=rows_k: total_ref.at[0, rows_k], totals, k)
     before[pl.ds(me, 1)] = payload[pl.ds(me, 1)]
     totals[pl.ds(me, 1)] = total_ref[...]
     rrows = lax.broadcasted_iota(jnp.int32, (rq.shape[0], rq.shape[0]), 0)
@@ -160,17 +166,19 @@
         col_seg = col_seg + (rcols >= end).astype(jnp.int32)
     heads_inner(rq, rk, rv, (row_seg == col_seg) & (rcols <= rrows), resp_inner)
 
-    wait_all(1, before)
+    wait_all(2, before, 0)
+    wait_all(3, before, 1)
     heads_finish(
         cq, cat_inner, lambda i: head_state(before, i, 0, half), gain_ref,
         side * cq.shape[1], 0, heads_here, cat_out,
     )
-    wait_all(2, totals)
+    wait_all(4, totals, 0)
+    wait_all(5, totals, 1)
     partner = pltpu.make_async_remote_copy(
         src_ref=totals,
         dst_ref=partner_totals,
-        send_sem=sends.at[3],
-        recv_sem=recvs.at[3],
+        send_sem=sends.at[6],
+        recv_sem=recvs.at[6],
         device_id={"resp": 1 - side},
         device_id_type=mesh_ids,
     )
@@ -211,8 +219,8 @@
             pltpu.VMEM((peers, half, DH), jnp.float32),
             pltpu.VMEM(cat[0].shape, jnp.float32),
             pltpu.VMEM(resp[0].shape, jnp.float32),
-            pltpu.SemaphoreType.DMA((4,)),
-            pltpu.SemaphoreType.DMA((4,)),
+            pltpu.SemaphoreType.DMA((7,)),
+            pltpu.SemaphoreType.DMA((7,)),
         ],
         compiler_params=pltpu.CompilerParams(collective_id=0, has_side_effects=True),
         cost_estimate=pl.CostEstimate(

time: 98.3 us -> 94.7 us (0.963)
  Pallas kernels: 94.6 us -> 91 us
    pallas_call x1, Pallas kernels: 94.6 us -> 91 us  [layer(): pl.pallas_call(layer_kernel, out_shape=(jax.ShapeDtypeStruct(cat[0].shape...]
where the time goes in v12:
time: 94.7 us; the launch traced here: 94.6 us
  Pallas kernels  91 us (96%)
  local copies, waits for them, and re-layouts  2.94 us (3%)
    pallas_call x1, Pallas kernels, layer(): pl.pallas_call(layer_kernel, out_shape=(jax.ShapeDtypeStruct(cat[0].shape...  91 us
    unnamed x4, local copies, waits for them, and re-layouts  2.94 us

profile of v12, /device:TPU:1, one launch (start us, length us, event | category | flops | bytes accessed | tf_op | source)
XLA Modules:
  0.0 94.6 jit_solution(6545406826179518794)
XLA Ops:
  0.6 91.0 %shard_map.95 = (bf16[128,2048]{1,0:T(8,128)(2,1)}, bf16[128,4096]{1,0:T(8,128)(2,1)}) custom-call(bf16[128,2048]{1,0:T(8,128)(2,1)} %cq.1, bf16[128,2048]{1,0:T(8,128)(2,1)} %ck.1, bf16[128,2048]{1,0:T(8,128)(2,1)} %cv.1, bf16[128,4096]{1,0:T(8,128)(2,1)} %rq.1, bf16[128,4096]{1,0:T(8,128)(2,1)} %rk.1, bf16[128,4096]{1,0:T(8,128)(2,1)} %rv.1, ...), custom_call_target="tpu_custom_call" | custom-call | flops 1006632960 | bytes 3670016 | tf_op jit(solution)/shard_map/pallas_call | solution.py:204
  91.6 0.0 copy-start
  91.6 2.0 %copy.12 = bf16[128,2048]{1,0:T(8,128)(2,1)} copy(bf16[128,2048]{1,0:T(8,128)(2,1)} %get-tuple-element.4) | data formatting | bytes 1048576
  93.6 0.0 copy-done
  93.6 1.0 %copy.13 = bf16[128,4096]{1,0:T(8,128)(2,1)} copy(bf16[128,4096]{1,0:T(8,128)(2,1)S(1)} %copy-done) | data formatting | bytes 2097152
Async XLA Ops:
  91.6 2.0 %copy-start = (bf16[128,4096]{1,0:T(8,128)(2,1)S(1)}, bf16[128,4096]{1,0:T(8,128)(2,1)}, u32[]{:S(2)}) copy-start(bf16[128,4096]{1,0:T(8,128)(2,1)} %get-tuple-element.5) | copy-start | bytes 3145732

commit v13 on v12

--- a/solution.py
+++ b/solution.py
@@ -7,6 +7,7 @@
 
 DH = 128
 UNROLL = 8
+PARTS = 4
 
 
 def block_state(key, value, heads):
@@ -103,7 +104,7 @@
     lax.fori_loop(0, heads_here, own_state, 0, unroll=UNROLL)
     pl.semaphore_wait(barrier, peers)
 
-    part = half // 2
+    part = half // PARTS
 
     def start_all(phase, src_of, dst, k):
         def start(t, carry):
@@ -133,14 +134,14 @@
         everyone.wait_send()
         everyone.wait_recv()
 
-    for k in range(2):
+    for k in range(PARTS):
         start_all(k, lambda peer, k=k: x_ref.at[peer, pl.ds(k * part, part)], got, k)
     got[pl.ds(me, 1)] = x_ref[pl.ds(me, 1)]
     rows = lax.broadcasted_iota(jnp.int32, (cq.shape[0], cq.shape[0]), 0)
     cols = lax.broadcasted_iota(jnp.int32, (cq.shape[0], cq.shape[0]), 1)
     heads_inner(cq, ck, cv, cols <= rows, cat_inner)
 
-    for k in range(2):
+    for k in range(PARTS):
         wait_all(k, got, k)
         rows_k = pl.ds(k * part, part)
 
@@ -151,8 +152,8 @@
         total_ref[:, rows_k] = lax.fori_loop(
             0, peers, running, jnp.zeros((part, DH), jnp.float32), unroll=8
         )[None]
-        start_all(2 + k, lambda peer, rows_k=rows_k: payload.at[peer, rows_k], before, k)
-        start_all(4 + k, lambda peer, rows_k=rows_k: total_ref.at[0, rows_k], totals, k)
+        start_all(PARTS + k, lambda peer, rows_k=rows_k: payload.at[peer, rows_k], before, k)
+        start_all(2 * PARTS + k, lambda peer, rows_k=rows_k: total_ref.at[0, rows_k], totals, k)
     before[pl.ds(me, 1)] = payload[pl.ds(me, 1)]
     totals[pl.ds(me, 1)] = total_ref[...]
     rrows = lax.broadcasted_iota(jnp.int32, (rq.shape[0], rq.shape[0]), 0)
@@ -166,19 +167,19 @@
         col_seg = col_seg + (rcols >= end).astype(jnp.int32)
     heads_inner(rq, rk, rv, (row_seg == col_seg) & (rcols <= rrows), resp_inner)
 
-    wait_all(2, before, 0)
-    wait_all(3, before, 1)
+    for k in range(PARTS):
+        wait_all(PARTS + k, before, k)
     heads_finish(
         cq, cat_inner, lambda i: head_state(before, i, 0, half), gain_ref,
         side * cq.shape[1], 0, heads_here, cat_out,
     )
-    wait_all(4, totals, 0)
-    wait_all(5, totals, 1)
+    for k in range(PARTS):
+        wait_all(2 * PARTS + k, totals, k)
     partner = pltpu.make_async_remote_copy(
         src_ref=totals,
         dst_ref=partner_totals,
-        send_sem=sends.at[6],
-        recv_sem=recvs.at[6],
+        send_sem=sends.at[3 * PARTS],
+        recv_sem=recvs.at[3 * PARTS],
         device_id={"resp": 1 - side},
         device_id_type=mesh_ids,
     )
@@ -219,8 +220,8 @@
             pltpu.VMEM((peers, half, DH), jnp.float32),
             pltpu.VMEM(cat[0].shape, jnp.float32),
             pltpu.VMEM(resp[0].shape, jnp.float32),
-            pltpu.SemaphoreType.DMA((7,)),
-            pltpu.SemaphoreType.DMA((7,)),
+            pltpu.SemaphoreType.DMA((3 * PARTS + 1,)),
+            pltpu.SemaphoreType.DMA((3 * PARTS + 1,)),
         ],
         compiler_params=pltpu.CompilerParams(collective_id=0, has_side_effects=True),
         cost_estimate=pl.CostEstimate(

time: 94.7 us -> 95.3 us (level)
  no operation moved by 1% of the time
where the time goes in v13:
time: 95.3 us; the launch traced here: 95.2 us
  Pallas kernels  91.6 us (96%)
  local copies, waits for them, and re-layouts  2.94 us (3%)
    pallas_call x1, Pallas kernels, layer(): pl.pallas_call(layer_kernel, out_shape=(jax.ShapeDtypeStruct(cat[0].shape...  91.6 us
    unnamed x4, local copies, waits for them, and re-layouts  2.94 us

profile of v13, /device:TPU:1, one launch (start us, length us, event | category | flops | bytes accessed | tf_op | source)
XLA Modules:
  0.0 95.2 jit_solution(16435032504959009361)
XLA Ops:
  0.6 91.6 %shard_map.95 = (bf16[128,2048]{1,0:T(8,128)(2,1)}, bf16[128,4096]{1,0:T(8,128)(2,1)}) custom-call(bf16[128,2048]{1,0:T(8,128)(2,1)} %cq.1, bf16[128,2048]{1,0:T(8,128)(2,1)} %ck.1, bf16[128,2048]{1,0:T(8,128)(2,1)} %cv.1, bf16[128,4096]{1,0:T(8,128)(2,1)} %rq.1, bf16[128,4096]{1,0:T(8,128)(2,1)} %rk.1, bf16[128,4096]{1,0:T(8,128)(2,1)} %rv.1, ...), custom_call_target="tpu_custom_call" | custom-call | flops 1006632960 | bytes 3670016 | tf_op jit(solution)/shard_map/pallas_call | solution.py:205
  92.3 0.0 copy-start
  92.3 2.0 %copy.12 = bf16[128,2048]{1,0:T(8,128)(2,1)} copy(bf16[128,2048]{1,0:T(8,128)(2,1)} %get-tuple-element.4) | data formatting | bytes 1048576
  94.2 0.0 copy-done
  94.2 1.0 %copy.13 = bf16[128,4096]{1,0:T(8,128)(2,1)} copy(bf16[128,4096]{1,0:T(8,128)(2,1)S(1)} %copy-done) | data formatting | bytes 2097152
Async XLA Ops:
  92.3 2.0 %copy-start = (bf16[128,4096]{1,0:T(8,128)(2,1)S(1)}, bf16[128,4096]{1,0:T(8,128)(2,1)}, u32[]{:S(2)}) copy-start(bf16[128,4096]{1,0:T(8,128)(2,1)} %get-tuple-element.5) | copy-start | bytes 3145732

commit v14 on v12

--- a/solution.py
+++ b/solution.py
@@ -151,8 +151,8 @@
         total_ref[:, rows_k] = lax.fori_loop(
             0, peers, running, jnp.zeros((part, DH), jnp.float32), unroll=8
         )[None]
+        start_all(4 + k, lambda peer, rows_k=rows_k: total_ref.at[0, rows_k], totals, k)
         start_all(2 + k, lambda peer, rows_k=rows_k: payload.at[peer, rows_k], before, k)
-        start_all(4 + k, lambda peer, rows_k=rows_k: total_ref.at[0, rows_k], totals, k)
     before[pl.ds(me, 1)] = payload[pl.ds(me, 1)]
     totals[pl.ds(me, 1)] = total_ref[...]
     rrows = lax.broadcasted_iota(jnp.int32, (rq.shape[0], rq.shape[0]), 0)
@@ -166,12 +166,6 @@
         col_seg = col_seg + (rcols >= end).astype(jnp.int32)
     heads_inner(rq, rk, rv, (row_seg == col_seg) & (rcols <= rrows), resp_inner)
 
-    wait_all(2, before, 0)
-    wait_all(3, before, 1)
-    heads_finish(
-        cq, cat_inner, lambda i: head_state(before, i, 0, half), gain_ref,
-        side * cq.shape[1], 0, heads_here, cat_out,
-    )
     wait_all(4, totals, 0)
     wait_all(5, totals, 1)
     partner = pltpu.make_async_remote_copy(
@@ -192,6 +186,12 @@
     heads_finish(
         rq, resp_inner, lambda i: head_state(partner_totals, i, 0, half), gain_ref,
         0, (1 - side) * heads_here, heads_here, resp_out,
+    )
+    wait_all(2, before, 0)
+    wait_all(3, before, 1)
+    heads_finish(
+        cq, cat_inner, lambda i: head_state(before, i, 0, half), gain_ref,
+        side * cq.shape[1], 0, heads_here, cat_out,
     )
 
 

time: 94.7 us -> 90.9 us (0.960)
  Pallas kernels: 91 us -> 87.2 us
    pallas_call x1, Pallas kernels: 91 us -> 87.2 us  [layer(): pl.pallas_call(layer_kernel, out_shape=(jax.ShapeDtypeStruct(cat[0].shape...]
where the time goes in v14:
time: 90.9 us; the launch traced here: 90.8 us
  Pallas kernels  87.2 us (96%)
  local copies, waits for them, and re-layouts  2.94 us (3%)
    pallas_call x1, Pallas kernels, layer(): pl.pallas_call(layer_kernel, out_shape=(jax.ShapeDtypeStruct(cat[0].shape...  87.2 us
    unnamed x4, local copies, waits for them, and re-layouts  2.94 us

profile of v14, /device:TPU:1, one launch (start us, length us, event | category | flops | bytes accessed | tf_op | source)
XLA Modules:
  0.0 90.8 jit_solution(8181062765790052042)
XLA Ops:
  0.6 87.2 %shard_map.95 = (bf16[128,2048]{1,0:T(8,128)(2,1)}, bf16[128,4096]{1,0:T(8,128)(2,1)}) custom-call(bf16[128,2048]{1,0:T(8,128)(2,1)} %cq.1, bf16[128,2048]{1,0:T(8,128)(2,1)} %ck.1, bf16[128,2048]{1,0:T(8,128)(2,1)} %cv.1, bf16[128,4096]{1,0:T(8,128)(2,1)} %rq.1, bf16[128,4096]{1,0:T(8,128)(2,1)} %rk.1, bf16[128,4096]{1,0:T(8,128)(2,1)} %rv.1, ...), custom_call_target="tpu_custom_call" | custom-call | flops 1006632960 | bytes 3670016 | tf_op jit(solution)/shard_map/pallas_call | solution.py:204
  87.9 0.0 copy-start
  87.9 2.0 %copy.12 = bf16[128,2048]{1,0:T(8,128)(2,1)} copy(bf16[128,2048]{1,0:T(8,128)(2,1)} %get-tuple-element.4) | data formatting | bytes 1048576
  89.8 0.0 copy-done
  89.8 1.0 %copy.13 = bf16[128,4096]{1,0:T(8,128)(2,1)} copy(bf16[128,4096]{1,0:T(8,128)(2,1)S(1)} %copy-done) | data formatting | bytes 2097152
Async XLA Ops:
  87.9 2.0 %copy-start = (bf16[128,4096]{1,0:T(8,128)(2,1)S(1)}, bf16[128,4096]{1,0:T(8,128)(2,1)}, u32[]{:S(2)}) copy-start(bf16[128,4096]{1,0:T(8,128)(2,1)} %get-tuple-element.5) | copy-start | bytes 3145732

commit v15 on v14

--- a/solution.py
+++ b/solution.py
@@ -166,23 +166,26 @@
         col_seg = col_seg + (rcols >= end).astype(jnp.int32)
     heads_inner(rq, rk, rv, (row_seg == col_seg) & (rcols <= rrows), resp_inner)
 
-    wait_all(4, totals, 0)
-    wait_all(5, totals, 1)
-    partner = pltpu.make_async_remote_copy(
-        src_ref=totals,
-        dst_ref=partner_totals,
-        send_sem=sends.at[6],
-        recv_sem=recvs.at[6],
-        device_id={"resp": 1 - side},
-        device_id_type=mesh_ids,
-    )
-    partner.start()
+    forwards = []
+    for k in range(2):
+        wait_all(4 + k, totals, k)
+        forward = pltpu.make_async_remote_copy(
+            src_ref=totals.at[:, pl.ds(k * part, part)],
+            dst_ref=partner_totals.at[:, pl.ds(k * part, part)],
+            send_sem=sends.at[6 + k],
+            recv_sem=recvs.at[6 + k],
+            device_id={"resp": 1 - side},
+            device_id_type=mesh_ids,
+        )
+        forward.start()
+        forwards.append(forward)
     heads_finish(
         rq, resp_inner, lambda i: head_state(totals, i, 0, half), gain_ref,
         0, side * heads_here, heads_here, resp_out,
     )
-    partner.wait_send()
-    partner.wait_recv()
+    for forward in forwards:
+        forward.wait_send()
+        forward.wait_recv()
     heads_finish(
         rq, resp_inner, lambda i: head_state(partner_totals, i, 0, half), gain_ref,
         0, (1 - side) * heads_here, heads_here, resp_out,
@@ -219,8 +222,8 @@
             pltpu.VMEM((peers, half, DH), jnp.float32),
             pltpu.VMEM(cat[0].shape, jnp.float32),
             pltpu.VMEM(resp[0].shape, jnp.float32),
-            pltpu.SemaphoreType.DMA((7,)),
-            pltpu.SemaphoreType.DMA((7,)),
+            pltpu.SemaphoreType.DMA((8,)),
+            pltpu.SemaphoreType.DMA((8,)),
         ],
         compiler_params=pltpu.CompilerParams(collective_id=0, has_side_effects=True),
         cost_estimate=pl.CostEstimate(

time: 90.9 us -> 90.9 us (level)
  no operation moved by 1% of the time
where the time goes in v15:
time: 90.9 us; the launch traced here: 90.8 us
  Pallas kernels  87.2 us (96%)
  local copies, waits for them, and re-layouts  2.94 us (3%)
    pallas_call x1, Pallas kernels, layer(): pl.pallas_call(layer_kernel, out_shape=(jax.ShapeDtypeStruct(cat[0].shape...  87.2 us
    unnamed x4, local copies, waits for them, and re-layouts  2.94 us

profile of v15, /device:TPU:1, one launch (start us, length us, event | category | flops | bytes accessed | tf_op | source)
XLA Modules:
  0.0 90.8 jit_solution(6964834500550951010)
XLA Ops:
  0.6 87.2 %shard_map.95 = (bf16[128,2048]{1,0:T(8,128)(2,1)}, bf16[128,4096]{1,0:T(8,128)(2,1)}) custom-call(bf16[128,2048]{1,0:T(8,128)(2,1)} %cq.1, bf16[128,2048]{1,0:T(8,128)(2,1)} %ck.1, bf16[128,2048]{1,0:T(8,128)(2,1)} %cv.1, bf16[128,4096]{1,0:T(8,128)(2,1)} %rq.1, bf16[128,4096]{1,0:T(8,128)(2,1)} %rk.1, bf16[128,4096]{1,0:T(8,128)(2,1)} %rv.1, ...), custom_call_target="tpu_custom_call" | custom-call | flops 1006632960 | bytes 3670016 | tf_op jit(solution)/shard_map/pallas_call | solution.py:207
  87.9 0.0 copy-start
  87.9 2.0 %copy.12 = bf16[128,2048]{1,0:T(8,128)(2,1)} copy(bf16[128,2048]{1,0:T(8,128)(2,1)} %get-tuple-element.4) | data formatting | bytes 1048576
  89.9 0.0 copy-done
  89.9 1.0 %copy.13 = bf16[128,4096]{1,0:T(8,128)(2,1)} copy(bf16[128,4096]{1,0:T(8,128)(2,1)S(1)} %copy-done) | data formatting | bytes 2097152
Async XLA Ops:
  87.9 2.0 %copy-start = (bf16[128,4096]{1,0:T(8,128)(2,1)S(1)}, bf16[128,4096]{1,0:T(8,128)(2,1)}, u32[]{:S(2)}) copy-start(bf16[128,4096]{1,0:T(8,128)(2,1)} %get-tuple-element.5) | copy-start | bytes 3145732

commit v16 on v14

--- a/solution.py
+++ b/solution.py
@@ -6,7 +6,7 @@
 from jax.sharding import PartitionSpec as P
 
 DH = 128
-UNROLL = 8
+UNROLL = 16
 
 
 def block_state(key, value, heads):

time: 90.9 us -> 90.3 us (level)
  no operation moved by 1% of the time
where the time goes in v16:
time: 90.3 us; the launch traced here: 90.2 us
  Pallas kernels  86.6 us (96%)
  local copies, waits for them, and re-layouts  2.94 us (3%)
    pallas_call x1, Pallas kernels, layer(): pl.pallas_call(layer_kernel, out_shape=(jax.ShapeDtypeStruct(cat[0].shape...  86.6 us
    unnamed x4, local copies, waits for them, and re-layouts  2.94 us

profile of v16, /device:TPU:1, one launch (start us, length us, event | category | flops | bytes accessed | tf_op | source)
XLA Modules:
  0.0 90.2 jit_solution(10470081749500249701)
XLA Ops:
  0.6 86.6 %shard_map.95 = (bf16[128,2048]{1,0:T(8,128)(2,1)}, bf16[128,4096]{1,0:T(8,128)(2,1)}) custom-call(bf16[128,2048]{1,0:T(8,128)(2,1)} %cq.1, bf16[128,2048]{1,0:T(8,128)(2,1)} %ck.1, bf16[128,2048]{1,0:T(8,128)(2,1)} %cv.1, bf16[128,4096]{1,0:T(8,128)(2,1)} %rq.1, bf16[128,4096]{1,0:T(8,128)(2,1)} %rk.1, bf16[128,4096]{1,0:T(8,128)(2,1)} %rv.1, ...), custom_call_target="tpu_custom_call" | custom-call | flops 1006632960 | bytes 3670016 | tf_op jit(solution)/shard_map/pallas_call | solution.py:204
  87.3 0.0 copy-start
  87.3 2.0 %copy.12 = bf16[128,2048]{1,0:T(8,128)(2,1)} copy(bf16[128,2048]{1,0:T(8,128)(2,1)} %get-tuple-element.4) | data formatting | bytes 1048576
  89.2 0.0 copy-done
  89.2 1.0 %copy.13 = bf16[128,4096]{1,0:T(8,128)(2,1)} copy(bf16[128,4096]{1,0:T(8,128)(2,1)S(1)} %copy-done) | data formatting | bytes 2097152
Async XLA Ops:
  87.3 2.0 %copy-start = (bf16[128,4096]{1,0:T(8,128)(2,1)S(1)}, bf16[128,4096]{1,0:T(8,128)(2,1)}, u32[]{:S(2)}) copy-start(bf16[128,4096]{1,0:T(8,128)(2,1)} %get-tuple-element.5) | copy-start | bytes 3145732
